TPU v7x, 512 devices: a whole 4x4x16 slice. The times are simulated.
512 devices in a mesh: tm: 64 (over y, z), head: 8 (over x, core).
Axes of the slice: x: 4, y: 4, z: 16, core: 2. Of those that a mesh axis runs over, the one named last changes fastest.
Arguments:
- queries: bfloat16 [8192, 4096], P('tm', 'head'), may hold values from -6 to 6
- keys: bfloat16 [8192, 4096], P('tm', 'head'), may hold values from -6 to 6
- values: bfloat16 [8192, 4096], P('tm', 'head'), may hold values from -6 to 6
- log_decay: float32 [32, 8192], P('head', 'tm'), may hold values from -1 to 0
- agent_ids: int32 [8192], P('tm'), may hold values from 0 to 127
- norm_gain: float32 [4096], P('head'), may hold values from 0.1 to 1.9
- out_grad: bfloat16 [8192, 4096], P('tm', 'head'), may hold values from -6 to 6
Outputs:
- result: bfloat16 [8192, 4096], P('tm', 'head')
- query_grad: bfloat16 [8192, 4096], P('tm', 'head')
- key_grad: bfloat16 [8192, 4096], P('tm', 'head')
- value_grad: bfloat16 [8192, 4096], P('tm', 'head')
- decay_grad: float32 [32, 8192], P('head', 'tm')
- gain_grad: float32 [4096], P('head')
All inputs are finite; a program needn't handle non-finite values.
Results may differ from a plain program's by a relative error of at most 0.001.
Values sent between devices are 32-bit elements; how exact they have to be, the bound alone decides.
No kernel may reach another device: no remote copies, remote signals or barrier semaphores. Data moves between devices by JAX's collectives and lax.ppermute only.
A program may use at most 128 MiB of HBM per device.

v0:
```python
import jax
import jax.numpy as jnp
from jax import lax
from jax.sharding import PartitionSpec as P

DK = 128
GROUP = 128
TEAM = 16
WIDTH = 4096


EPS = 1e-06
HIGH = lax.Precision.HIGHEST


def entering(value, axis, join, neutral, backward):
    count, mine = (lax.axis_size(axis), lax.axis_index(axis))
    pieces = jax.tree.map(lambda part: lax.all_gather(part, axis), value)
    if backward:
        pieces = jax.tree.map(lambda part: part[::-1], pieces)
        mine = count - 1 - mine
    subtotal = jax.tree.map(
        lambda part, zero: jnp.full_like(part, 0) + jnp.asarray(zero, part.dtype), value, neutral
    )

    def turn(position, subtotal):
        longer = join(subtotal, jax.tree.map(lambda part: part[position], pieces))
        return jax.tree.map(lambda new, old: jnp.where(position < mine, new, old), longer, subtotal)

    return lax.fori_loop(0, count - 1, turn, subtotal)


def group_pass(scaled, key_rows, value_rows, decays, teams):
    length, heads, depth = scaled.shape
    blocks = length // GROUP
    query_blocks = scaled.reshape(blocks, GROUP, heads, depth)
    key_blocks = key_rows.reshape(blocks, GROUP, heads, depth)
    value_blocks = value_rows.reshape(blocks, GROUP, heads, depth)
    decay_blocks = decays.reshape(heads, blocks, GROUP).transpose(1, 0, 2)
    team_blocks = teams.reshape(blocks, GROUP)
    places = jnp.arange(GROUP)
    causal = places[:, None] >= places[None, :]

    def advance(state, inputs):
        query_block, key_block, value_block, decay_block, team_block = inputs
        cumulative = jnp.cumsum(decay_block, axis=1)
        visible = (causal & (team_block[:, None] == team_block[None, :]))[None]
        spread = cumulative[:, :, None] - cumulative[:, None, :]
        weights = jnp.where(visible, jnp.exp(jnp.where(visible, spread, 0.0)), 0.0)
        scores = jnp.einsum("thd,shd->hts", query_block, key_block, precision=HIGH) * weights
        output = jnp.einsum("hts,she->the", scores, value_block, precision=HIGH)
        carried = jnp.einsum("thd,hde->the", query_block, state, precision=HIGH)
        output = output + jnp.exp(cumulative).T[:, :, None] * carried
        tail = jnp.exp(cumulative[:, -1:] - cumulative)
        fresh = jnp.einsum(
            "shd,she->hde", key_block * tail.T[:, :, None], value_block, precision=HIGH
        )
        state = jnp.exp(cumulative[:, -1])[:, None, None] * state + fresh
        return (state, output)

    start = jnp.zeros((heads, depth, depth), jnp.float32)
    final, outputs = lax.scan(
        advance, start, (query_blocks, key_blocks, value_blocks, decay_blocks, team_blocks)
    )
    return (outputs.reshape(length, heads, depth), final)


def combine(earlier, later):
    return (earlier[0] * later[0], later[0][:, None, None] * earlier[1] + later[1])


def body(queries, keys, values, log_decay, agent_ids, norm_gain, out_grad):
    length = queries.shape[0]
    heads_here = queries.shape[1] // DK
    factor_q = DK ** (-0.5)
    scaled = queries.astype(jnp.float32).reshape(length, heads_here, DK) * factor_q
    key_rows = keys.astype(jnp.float32).reshape(length, heads_here, DK)
    value_rows = values.astype(jnp.float32).reshape(length, heads_here, DK)
    teams = agent_ids // TEAM

    def local_pass(query_in, key_in, value_in, decays):
        return group_pass(query_in, key_in, value_in, decays, teams)

    (local_out, local_end), pullback = jax.vjp(local_pass, scaled, key_rows, value_rows, log_decay)
    cumulative = jnp.cumsum(log_decay, axis=1)
    factor = jnp.exp(cumulative[:, -1])
    unit = (jnp.ones((heads_here,), jnp.float32), jnp.zeros((heads_here, DK, DK), jnp.float32))
    state_in = entering((factor, local_end), "tm", combine, unit, False)[1]
    inter_term = jnp.einsum("thd,hde->the", scaled, state_in, precision=HIGH)
    weights = jnp.exp(cumulative).T[:, :, None]
    output = local_out + weights * inter_term
    flat = output.reshape(length, heads_here * DK)
    grad_rows = out_grad.astype(jnp.float32)
    scaled_grad = grad_rows * norm_gain
    square_part = jnp.sum(flat * flat, axis=1)
    square_sum = lax.psum(square_part, "head")
    rms_value = jnp.sqrt(square_sum / WIDTH + EPS)
    normed = flat / rms_value[:, None]
    result = (normed * norm_gain).astype(jnp.bfloat16)
    inner_sum = lax.psum(jnp.sum(scaled_grad * flat, axis=1), "head")
    gain_grad = lax.psum(jnp.sum(grad_rows * normed, axis=0), "tm")
    flat_grad = (
        scaled_grad / rms_value[:, None] - flat * (inner_sum / (WIDTH * rms_value**3))[:, None]
    )
    out_adjoint = flat_grad.reshape(length, heads_here, DK)
    weighted = out_adjoint * weights
    own_adjoint = jnp.einsum("thd,the->hde", scaled, weighted, precision=HIGH)
    end_adjoint = entering((factor, own_adjoint), "tm", combine, unit, True)[1]
    query_part, key_part, value_part, decay_part = pullback((out_adjoint, end_adjoint))
    query_total = query_part + weights * jnp.einsum(
        "the,hde->thd", out_adjoint, state_in, precision=HIGH
    )
    reach = jnp.sum(weights * inter_term * out_adjoint, axis=2).T
    reach_back = jnp.flip(jnp.cumsum(jnp.flip(reach, 1), axis=1), 1)
    through_end = factor * jnp.sum(end_adjoint * state_in, axis=(1, 2))
    decay_grad = decay_part + reach_back + through_end[:, None]
    query_grad = (query_total * factor_q).reshape(length, heads_here * DK).astype(jnp.bfloat16)
    key_grad = key_part.reshape(length, heads_here * DK).astype(jnp.bfloat16)
    value_grad = value_part.reshape(length, heads_here * DK).astype(jnp.bfloat16)
    return (result, query_grad, key_grad, value_grad, decay_grad, gain_grad)


def solution(mesh):
    placed = (
        P("tm", "head"),
        P("tm", "head"),
        P("tm", "head"),
        P("head", "tm"),
        P("tm"),
        P("head"),
        P("tm", "head"),
    )
    return jax.shard_map(
        body,
        mesh=mesh,
        in_specs=placed,
        out_specs=(
            P("tm", "head"),
            P("tm", "head"),
            P("tm", "head"),
            P("tm", "head"),
            P("head", "tm"),
            P("head"),
        ),
        check_vma=False,
    )
```

profile of v0, /device:TPU:1, one launch (start us, length us, event | category | flops | bytes accessed | tf_op | source)
XLA Modules:
  0.0 592.1 jit_solution(4932843681317344914)
XLA Ops:
  10.6 1.3 dynamic-slice.1
  12.8 123.9 %all-reduce.2 = f32[256]{0:T(256)S(1)} all-reduce(f32[256]{0:T(256)S(1)} %dynamic-update-slice), channel_id=2, replica_groups=mesh['tm'=64,'head'=8] {'tm'}, use_global_device_ids=true, to_apply=%add.2 | all-reduce | flops 256 | bytes 2048
  139.5 69.7 %all-gather.6.cloned.1.call-done = f32[256,128,128]{2,1,0:T(8,128)} async-done(((f32[4,128,128]{2,1,0:T(8,128)}), f32[256,128,128]{2,1,0:T(8,128)}) %all-gather.6.cloned.1.call-update) | async-done | bytes 16777232 | tf_op jit(solution)/shard_map/all_gather | solution.py:18
  209.2 69.1 %while.20 = (s32[]{:T(128)}, f32[4,128,128]{2,1,0:T(8,128)S(1)}, s32[]{:T(128)}, f32[64,4]{1,0:T(8,128)S(1)}, f32[64,4,128,128]{3,2,1,0:T(8,128)}, /*index=5*/s32[]{:T(128)}, s32[]{:T(128)}) while((s32[]{:T(128)}, f32[4,128,128]{2,1,0:T(8,128)S(1)}, s32[]{:T(128)}, f32[64,4]{1,0:T(8,128)S(1)}, f32[64,4,128,128]{3,2,1,0:T(8,128)}, ...), condition=%wide.region_2.3_spmd.clone, body=%wide.region_1.2_spmd.clone.sunk | while | flops 262148 | bytes 786593 | solution.py:30
  279.5 13.1 %psum.21 = f32[128]{0:T(128)S(1)} all-reduce(f32[128]{0:T(128)S(1)} %get-tuple-element.518), channel_id=1, replica_groups=mesh['tm'=64,'head'=8] {'head'}, use_global_device_ids=true, to_apply=%region_4.5 | all-reduce | flops 128 | bytes 1024 | tf_op jit(solution)/shard_map/psum | solution.py:96
  292.7 1.1 fusion.19
  293.8 13.9 %psum.22 = f32[128]{0:T(128)S(1)} all-reduce(f32[128]{0:T(128)S(1)} %get-tuple-element.485), channel_id=1, replica_groups=mesh['tm'=64,'head'=8] {'head'}, use_global_device_ids=true, to_apply=%region_6.7 | all-reduce | flops 128 | bytes 1024 | tf_op jit(solution)/shard_map/psum | solution.py:100
  307.7 1.7 fusion.16
  309.5 1.4 fusion.25
  314.1 113.8 %psum.23 = f32[512]{0:T(512)} all-reduce(f32[512]{0:T(512)S(1)} %get-tuple-element.484), channel_id=1, replica_groups=mesh['tm'=64,'head'=8] {'tm'}, use_global_device_ids=true, to_apply=%region_20.21 | all-reduce | flops 512 | bytes 4096 | tf_op jit(solution)/shard_map/psum | solution.py:101
  427.9 69.9 %all-gather.8.cloned.1.call-done = f32[256,128,128]{2,1,0:T(8,128)} async-done(((f32[4,128,128]{2,1,0:T(8,128)}), f32[256,128,128]{2,1,0:T(8,128)}) %all-gather.8.cloned.1.call-update) | async-done | bytes 16777232 | tf_op jit(solution)/shard_map/all_gather | solution.py:18
  497.8 11.6 %rev.14 = f32[64,4,128,128]{3,2,1,0:T(8,128)} reverse(f32[64,4,128,128]{3,2,1,0:T(8,128)} %bitcast.136), dimensions={0} | reverse | bytes 33554432 | tf_op jit(solution)/shard_map/rev | solution.py:20
  509.5 69.4 %while.21 = (s32[]{:T(128)}, f32[4,128,128]{2,1,0:T(8,128)S(1)}, s32[]{:T(128)}, f32[64,4]{1,0:T(8,128)S(1)}, f32[64,4,128,128]{3,2,1,0:T(8,128)}, /*index=5*/s32[]{:T(128)}, s32[]{:T(128)}) while((s32[]{:T(128)}, f32[4,128,128]{2,1,0:T(8,128)S(1)}, s32[]{:T(128)}, f32[64,4]{1,0:T(8,128)S(1)}, f32[64,4,128,128]{3,2,1,0:T(8,128)}, ...), condition=%wide.region_8.9_spmd.clone, body=%wide.region_7.8_spmd.clone.sunk | while | flops 262148 | bytes 786593 | solution.py:30
  510.6 1.1 fusion.103
  511.7 1.1 fusion.103
  512.8 1.1 fusion.103
  513.9 1.1 fusion.103
  518.3 1.1 fusion.103
  534.8 1.1 fusion.103
  539.2 1.1 fusion.103
  555.8 1.1 fusion.103
  560.2 1.1 fusion.103
  576.7 1.1 fusion.103
  583.3 1.3 reduce_window_sum.36
  (295 shorter events, 139.9 us)
Async XLA Ops:
  7.2 2.4 copy-start
  7.2 202.0 %all-gather.6.cloned.1.call-start = ((), (), s32[]{:S(2)}) async-start(), calls=%async_computation | async-start | bytes 17039360 | tf_op jit(solution)/shard_map/all_gather | solution.py:18
  10.5 487.3 %all-gather.8.cloned.1.call-start = ((), (), s32[]{:S(2)}) async-start(), calls=%async_computation.1 | async-start | bytes 17039360 | tf_op jit(solution)/shard_map/all_gather | solution.py:18
Sparse Core Ops, SparseCore 0:
  10.9 198.2 all-gather.5
  311.0 186.7 all-gather.7
where the time goes:
time: 596 us; the launch traced here: 592 us
  blocking collectives  265 us (44%)
  other arithmetic  142 us (24%)
  waiting for transfers between devices  140 us (23%)
  local copies, waits for them, and re-layouts  19 us (3%)
  between operations  14.9 us (2%)
  matrix products  8.1 us (1%)
    all_gather x2, waiting for transfers between devices, entering(): pieces = jax.tree.map(lambda part: lax.all_gather(part, axis), value)  140 us
    select_n x126, other arithmetic, turn(): jnp.where(position < mine, new, old)  133 us
    unnamed x1, blocking collectives  124 us
    psum x1, blocking collectives, body(): gain_grad = lax.psum(jnp.sum(grad_rows * normed, axis=0), 'tm')  114 us
    psum x1, blocking collectives, body(): inner_sum = lax.psum(jnp.sum(scaled_grad * flat, axis=1), 'head')  13.9 us
    psum x1, blocking collectives, body(): square_sum = lax.psum(square_part, 'head')  13.1 us
  transfers between devices with their start and end apart: 2, of which 2 were waited for; matrix products, arithmetic and copies ran while one was open for 1% of the time, Pallas kernels for 0%

commit v1 on v0

v1 whole, which is shorter than its diff:
```python
import functools

import jax
import jax.numpy as jnp
from jax import lax
from jax.experimental import pallas as pl
from jax.experimental.pallas import tpu as pltpu
from jax.sharding import PartitionSpec as P

DK = 128
STEPS = 128
HEADS = 4
TEAM = 16
WIDTH = 4096
EPS = 1e-06
SCALE = DK ** (-0.5)
Z = 16
Y = 4
ROWS = HEADS * DK // Z
F32 = jnp.float32
BF16 = jnp.bfloat16

NN = (((1,), (0,)), ((), ()))
NT = (((1,), (1,)), ((), ()))
TN = (((0,), (0,)), ((), ()))


def mm(a, b, dims):
    return lax.dot_general(a, b, dims, preferred_element_type=F32)


def exact(a, b, dims):
    return lax.dot_general(
        a, b, dims, precision=lax.Precision.HIGHEST, preferred_element_type=F32
    )


def parts(a):
    high = a.astype(BF16)
    return high, (a - high.astype(F32)).astype(BF16)


def wide_left(a, b, dims):
    high, low = parts(a)
    return mm(high, b, dims) + mm(low, b, dims)


def wide_right(a, b, dims):
    high, low = parts(b)
    return mm(a, high, dims) + mm(a, low, dims)


def wide_both(a, b, dims):
    ah, al = parts(a)
    bh, bl = parts(b)
    return mm(ah, bh, dims) + (mm(ah, bl, dims) + mm(al, bh, dims))


def grid_index():
    rows = lax.broadcasted_iota(jnp.int32, (STEPS, STEPS), 0)
    cols = lax.broadcasted_iota(jnp.int32, (STEPS, STEPS), 1)
    return rows, cols


def head(ref, h):
    return ref[:, h * DK : (h + 1) * DK]


def state_kernel(k_ref, v_ref, decay_ref, out_ref):
    rows, cols = grid_index()
    decay = decay_ref[...]
    after = exact((cols > rows).astype(F32), decay, NT)
    tail = jnp.exp(after)
    factor = jnp.exp(jnp.sum(decay, axis=1, keepdims=True))
    for h in range(HEADS):
        k = head(k_ref, h).astype(F32) * tail[:, h : h + 1]
        state = wide_left(k, head(v_ref, h), TN)
        for j in range(Z // HEADS):
            out_ref[h * (Z // HEADS) + j, :ROWS, :] = state[j * ROWS : (j + 1) * ROWS]
            out_ref[h * (Z // HEADS) + j, ROWS:, :] = jnp.broadcast_to(factor[h : h + 1], (8, DK))


def tiled(factor, value):
    return (value.reshape(ROWS // 8, 8, DK) * factor[None]).reshape(ROWS, DK)


def row_scan_kernel(backward, with_gain, *refs):
    if with_gain:
        in_ref, factor_ref, gain_ref, local_ref, row_ref = refs
    else:
        in_ref, local_ref, reach_ref, factor_ref, row_ref = refs
    order = range(Z - 1, -1, -1) if backward else range(Z)
    running = jnp.zeros((ROWS, DK), F32)
    product = jnp.ones((8, DK), F32)
    for z in order:
        factor = factor_ref[z] if with_gain else in_ref[z, ROWS:, :]
        local_ref[z] = running
        if not with_gain:
            reach_ref[z] = product
            factor_ref[z] = factor
        running = tiled(factor, running) + in_ref[z, :ROWS, :]
        product = product * factor
    extra = gain_ref[...] if with_gain else product
    for y in range(Y):
        row_ref[y, :ROWS, :] = running
        row_ref[y, ROWS:, :] = extra


def join_kernel(backward, with_gain, *refs):
    if with_gain:
        in_ref, local_ref, factor_ref, rows_ref, out_ref = refs
    else:
        in_ref, local_ref, reach_ref, out_ref = refs
    mine = lax.axis_index("tm") // Z
    running = jnp.zeros((ROWS, DK), F32)
    order = range(Y - 1, 0, -1) if backward else range(Y - 1)
    for y in order:
        factor = rows_ref[y, ROWS:, :] if with_gain else in_ref[y, ROWS:, :]
        longer = tiled(factor, running) + in_ref[y, :ROWS, :]
        use = (y > mine) if backward else (y < mine)
        running = jnp.where(use, longer, running)
    if with_gain:
        gain = in_ref[0, ROWS:, :]
        for y in range(1, Y):
            gain = gain + in_ref[y, ROWS:, :]
        product = jnp.ones((8, DK), F32)
        for z in range(Z - 1, -1, -1):
            out_ref[z, :ROWS, :] = local_ref[z] + tiled(product, running)
            out_ref[z, ROWS:, :] = gain
            product = product * factor_ref[z]
    else:
        for z in range(Z):
            out_ref[z] = local_ref[z] + tiled(reach_ref[z], running)


def decays(decay):
    rows, cols = grid_index()
    lower = (cols <= rows).astype(F32)
    column = exact(lower, decay, NT)
    row = exact(decay, lower, NT)
    return column, row


def weights_of(column, row, visible, h):
    spread = column[:, h : h + 1] - row[h : h + 1, :]
    return jnp.where(visible, jnp.exp(jnp.where(visible, spread, 0.0)), 0.0)


def visible_of(ids_ref):
    rows, cols = grid_index()
    team = jnp.broadcast_to((ids_ref[...] // TEAM).astype(F32), (STEPS, STEPS))
    return (cols <= rows) & (team == team.T)


def state_of(ref, h):
    per = Z // HEADS
    return jnp.concatenate([ref[h * per + j, :ROWS, :] for j in range(per)], axis=0)


def output_kernel(q_ref, k_ref, v_ref, decay_ref, ids_ref, gain_ref, grad_ref, state_ref, out_ref, sums_ref):
    column, row = decays(decay_ref[...])
    visible = visible_of(ids_ref)
    grown = jnp.exp(column)
    squares = jnp.zeros((STEPS, DK), F32)
    inners = jnp.zeros((STEPS, DK), F32)
    for h in range(HEADS):
        q, k, v = head(q_ref, h), head(k_ref, h), head(v_ref, h)
        scores = mm(q, k, NT) * (weights_of(column, row, visible, h) * SCALE)
        inter = wide_right(q, state_of(state_ref, h), NN)
        out = wide_left(scores, v, NN) + (grown[:, h : h + 1] * SCALE) * inter
        out_ref[:, h * DK : (h + 1) * DK] = out
        squares = squares + out * out
        inners = inners + head(grad_ref, h).astype(F32) * head(gain_ref, h) * out
    ones = jnp.ones((8, DK), F32)
    both = jnp.where(
        lax.broadcasted_iota(jnp.int32, (8, STEPS), 0) == 0,
        exact(ones, squares, NT),
        exact(ones, inners, NT),
    )
    for p in range(8):
        sums_ref[p] = both


def norm_kernel(sums_ref, o_ref, q_ref, decay_ref, gain_ref, grad_ref, result_ref, adjoint_ref, own_ref, part_ref):
    rows, cols = grid_index()
    total = sums_ref[0]
    for p in range(1, 8):
        total = total + sums_ref[p]
    total = total.T
    inverse = 1.0 / jnp.sqrt(total[:, 0:1] / WIDTH + EPS)
    pull = total[:, 1:2] * (inverse * inverse * inverse) / WIDTH
    grown = jnp.exp(exact((cols <= rows).astype(F32), decay_ref[...], NT)) * SCALE
    part_ref[...] = jnp.zeros((8, DK), F32)
    for h in range(HEADS):
        out = head(o_ref, h)
        gain = head(gain_ref, h)
        grad = head(grad_ref, h).astype(F32)
        normed = out * inverse
        result_ref[:, h * DK : (h + 1) * DK] = (normed * gain).astype(BF16)
        part_ref[h : h + 1, :] = jnp.sum(grad * normed, axis=0, keepdims=True)
        adjoint = grad * gain * inverse - out * pull
        adjoint_ref[:, h * DK : (h + 1) * DK] = adjoint
        own = wide_right(head(q_ref, h), adjoint * grown[:, h : h + 1], TN)
        for j in range(Z // HEADS):
            own_ref[h * (Z // HEADS) + j] = own[j * ROWS : (j + 1) * ROWS]


def final_kernel(
    q_ref, k_ref, v_ref, decay_ref, ids_ref, state_ref, adjoint_ref, end_ref,
    dq_ref, dk_ref, dv_ref, dd_ref, dg_ref,
):
    decay = decay_ref[...]
    column, row = decays(decay)
    rows, cols = grid_index()
    visible = visible_of(ids_ref)
    grown = jnp.exp(column)
    tail = jnp.exp(exact((cols > rows).astype(F32), decay, NT))
    factor = jnp.exp(jnp.sum(decay, axis=1, keepdims=True))
    until = (rows >= cols).astype(F32)
    before = (rows < cols).astype(F32)
    for h in range(HEADS):
        span = slice(h * DK, (h + 1) * DK)
        q, k, v = head(q_ref, h), head(k_ref, h), head(v_ref, h)
        adjoint = head(adjoint_ref, h)
        state = state_of(state_ref, h)
        end = state_of(end_ref, h)
        weights = weights_of(column, row, visible, h) * SCALE
        scores = mm(q, k, NT) * weights
        slopes = wide_left(adjoint, v, NT)
        joint = scores * slopes
        slopes = slopes * weights
        inter = wide_both(adjoint, state, NT) * (grown[:, h : h + 1] * SCALE)
        dq_ref[:, span] = (wide_left(slopes, k, NN) + inter).astype(BF16)
        dk_end = wide_right(v, end, NT) * tail[:, h : h + 1]
        dk_ref[:, span] = (wide_left(slopes, q, TN) + dk_end).astype(BF16)
        dv_end = wide_right(k, end, NN) * tail[:, h : h + 1]
        dv_ref[:, span] = (wide_both(scores, adjoint, TN) + dv_end).astype(BF16)
        late = jnp.sum(joint + inter * q.astype(F32), axis=1, keepdims=True)
        early = jnp.sum(dk_end * k.astype(F32), axis=1, keepdims=True)
        columns = jnp.sum(joint, axis=0, keepdims=True)
        through = factor[h : h + 1] * jnp.sum(end * state)
        dd_ref[h : h + 1, :] = (
            jnp.sum(late * until, axis=0, keepdims=True)
            + jnp.sum(early * before, axis=0, keepdims=True)
            - exact(jnp.broadcast_to(columns, (8, STEPS)), until, NN)[0:1]
            + through
        )
    total = end_ref[0, ROWS:, :]
    for z in range(1, Z):
        total = total + end_ref[z, ROWS:, :]
    dg_ref[...] = total


def call(kernel, shapes, *arrays):
    return pl.pallas_call(
        kernel,
        out_shape=[jax.ShapeDtypeStruct(s, d) for s, d in shapes],
        in_specs=[pl.BlockSpec(memory_space=pltpu.VMEM)] * len(arrays),
        out_specs=[pl.BlockSpec(memory_space=pltpu.VMEM)] * len(shapes),
    )(*arrays)


Z_GROUPS = [[y * Z + z for z in range(Z)] for y in range(Y)]
Y_GROUPS = [[y * Z + z for y in range(Y)] for z in range(Z)]


def swap(value, axis, groups=None):
    return lax.all_to_all(value, axis, 0, 0, axis_index_groups=groups, tiled=True)


def body(queries, keys, values, log_decay, agent_ids, norm_gain, out_grad):
    ids = agent_ids.reshape(1, STEPS)
    gain = norm_gain.reshape(1, HEADS * DK)
    wide = (STEPS, HEADS * DK)
    slices, padded = (Z, ROWS, DK), (Z, ROWS + 8, DK)
    (ends,) = call(state_kernel, [(padded, F32)], keys, values, log_decay)
    ends = swap(ends, "tm", Z_GROUPS)
    local, reach, factors, row = call(
        functools.partial(row_scan_kernel, False, False),
        [(slices, F32), ((Z, 8, DK), F32), ((Z, 8, DK), F32), ((Y, ROWS + 8, DK), F32)],
        ends,
    )
    rows = swap(row, "tm", Y_GROUPS)
    (entering,) = call(functools.partial(join_kernel, False, False), [(slices, F32)], rows, local, reach)
    state = swap(entering, "tm", Z_GROUPS)
    out, sums = call(
        output_kernel,
        [(wide, F32), ((8, 8, STEPS), F32)],
        queries, keys, values, log_decay, ids, gain, out_grad, state,
    )
    sums = swap(sums, "head")
    result, adjoint, own, part = call(
        norm_kernel,
        [(wide, BF16), (wide, F32), (slices, F32), ((8, DK), F32)],
        sums, out, queries, log_decay, gain, out_grad,
    )
    own = swap(own, "tm", Z_GROUPS)
    local, row = call(
        functools.partial(row_scan_kernel, True, True),
        [(slices, F32), ((Y, ROWS + 8, DK), F32)],
        own, factors, part,
    )
    row = swap(row, "tm", Y_GROUPS)
    (leaving,) = call(functools.partial(join_kernel, True, True), [(padded, F32)], row, local, factors, rows)
    end = swap(leaving, "tm", Z_GROUPS)
    query_grad, key_grad, value_grad, decay_grad, gain_grad = call(
        final_kernel,
        [(wide, BF16), (wide, BF16), (wide, BF16), ((HEADS, STEPS), F32), ((8, DK), F32)],
        queries, keys, values, log_decay, ids, state, adjoint, end,
    )
    return result, query_grad, key_grad, value_grad, decay_grad, gain_grad[:HEADS].reshape(-1)


def solution(mesh):
    wide = P("tm", "head")
    return jax.shard_map(
        body,
        mesh=mesh,
        in_specs=(wide, wide, wide, P("head", "tm"), P("tm"), P("head"), wide),
        out_specs=(wide, wide, wide, wide, P("head", "tm"), P("head")),
        check_vma=False,
    )
```

time: 596 us -> 160 us (0.27)
  the two profiles are of different devices: /device:TPU:1 before, /device:TPU:32 now
where the time goes in v1:
time: 160 us; the launch traced here: 159 us
  blocking collectives  138 us (86%)
  Pallas kernels  18.7 us (12%)
    all_to_all x7, blocking collectives, swap(): lax.all_to_all(value, axis, 0, 0, axis_index_groups=groups, tiled=True)  138 us
    pallas_call x8, Pallas kernels, call(): pl.pallas_call(kernel, out_shape=[jax.ShapeDtypeStruct(s, d) for s, d in...  18.7 us

profile of v1, /device:TPU:32, one launch (start us, length us, event | category | flops | bytes accessed | tf_op | source)
XLA Modules:
  0.0 158.8 jit_solution(8374955984383602082)
XLA Ops:
  0.6 2.3 %shard_map.118 = f32[16,40,128]{2,1,0:T(8,128)} custom-call(bf16[128,512]{1,0:T(8,128)(2,1)} %k_ref.5, bf16[128,512]{1,0:T(8,128)(2,1)} %v_ref.5, f32[4,128]{1,0:T(4,128)} %decay_ref.7), custom_call_target="tpu_custom_call" | custom-call | tf_op jit(solution)/shard_map/pallas_call | solution.py:255
  3.0 35.2 %all_to_all.35.refs_0_ = f32[16,40,128]{2,1,0:T(8,128)} all-to-all(f32[16,40,128]{2,1,0:T(8,128)} %shard_map.118), channel_id=1, replica_groups={{0,8,16,24,32,40,48,56,64,72,80,88,96,104,112,120},{128,136,144,152,160..., dimensions={0} | all-to-all | bytes 655360 | tf_op jit(solution)/shard_map/all_to_all | solution.py:268
  38.2 1.8 %shard_map.119 = (f32[16,32,128]{2,1,0:T(8,128)}, f32[16,8,128]{2,1,0:T(8,128)}, f32[16,8,128]{2,1,0:T(8,128)}, f32[4,40,128]{2,1,0:T(8,128)}) custom-call(f32[16,40,128]{2,1,0:T(8,128)} %all_to_all.35.refs_0_), custom_call_target="tpu_custom_call" | custom-call | tf_op jit(solution)/shard_map/pallas_call | solution.py:255
  39.9 10.3 %all_to_all.36.refs_0_.refs_3_ = f32[4,40,128]{2,1,0:T(8,128)} all-to-all(f32[4,40,128]{2,1,0:T(8,128)} %get-tuple-element.23), channel_id=1, replica_groups={{0,128,256,384},{8,136,264,392},{16,144,272,400},{24,152,280,408},{32,1..., dimensions={0} | all-to-all | bytes 163840 | tf_op jit(solution)/shard_map/all_to_all | solution.py:268
  50.2 1.7 %shard_map.120 = f32[16,32,128]{2,1,0:T(8,128)} custom-call(f32[4,40,128]{2,1,0:T(8,128)} %all_to_all.36.refs_0_.refs_3_, f32[16,32,128]{2,1,0:T(8,128)} %get-tuple-element.24.refs_1_, f32[16,8,128]{2,1,0:T(8,128)} %get-tuple-element.25.refs_2_), custom_call_target="tpu_custom_call" | custom-call | tf_op jit(solution)/shard_map/pallas_call | solution.py:255
  51.9 24.7 %all_to_all.37.state_ref = f32[16,32,128]{2,1,0:T(8,128)} all-to-all(f32[16,32,128]{2,1,0:T(8,128)} %shard_map.120), channel_id=1, replica_groups={{0,8,16,24,32,40,48,56,64,72,80,88,96,104,112,120},{128,136,144,152,160..., dimensions={0} | all-to-all | bytes 524288 | tf_op jit(solution)/shard_map/all_to_all | solution.py:268
  76.6 3.1 %shard_map.121 = (f32[128,512]{1,0:T(8,128)}, f32[8,8,128]{2,1,0:T(8,128)}) custom-call(bf16[128,512]{1,0:T(8,128)(2,1)} %q_ref.5, bf16[128,512]{1,0:T(8,128)(2,1)} %k_ref.5, bf16[128,512]{1,0:T(8,128)(2,1)} %v_ref.5, f32[4,128]{1,0:T(4,128)} %decay_ref.7, s32[1,128]{1,0:T(1,128)} %bitcast.6, f32[1,512]{1,0:T(1,128)} %bitcast.4, bf16[128,512]{1,0:T(8,128)(2,1)} %grad_ref.3, ...), custom_call_target="tpu_custom_call" | custom-call | tf_op jit(solution)/shard_map/pallas_call | solution.py:255
  79.7 9.8 %all_to_all.38.sums_ref = f32[8,8,128]{2,1,0:T(8,128)} all-to-all(f32[8,8,128]{2,1,0:T(8,128)} %get-tuple-element.26), channel_id=1, replica_groups=mesh['tm'=64,'head'=8] {'head'}, dimensions={0} | all-to-all | bytes 65536 | tf_op jit(solution)/shard_map/all_to_all | solution.py:268
  89.6 2.4 %shard_map.122 = (bf16[128,512]{1,0:T(8,128)(2,1)}, f32[128,512]{1,0:T(8,128)}, f32[16,32,128]{2,1,0:T(8,128)}, f32[8,128]{1,0:T(8,128)}) custom-call(f32[8,8,128]{2,1,0:T(8,128)} %all_to_all.38.sums_ref, f32[128,512]{1,0:T(8,128)} %get-tuple-element.27.o_ref, bf16[128,512]{1,0:T(8,128)(2,1)} %q_ref.5, f32[4,128]{1,0:T(4,128)} %decay_ref.7, ...), custom_call_target="tpu_custom_call" | custom-call | tf_op jit(solution)/shard_map/pallas_call | solution.py:255
  92.0 22.7 %all_to_all.39.refs_0_ = f32[16,32,128]{2,1,0:T(8,128)} all-to-all(f32[16,32,128]{2,1,0:T(8,128)} %get-tuple-element.30), channel_id=1, replica_groups={{0,8,16,24,32,40,48,56,64,72,80,88,96,104,112,120},{128,136,144,152,160..., dimensions={0} | all-to-all | bytes 524288 | tf_op jit(solution)/shard_map/all_to_all | solution.py:268
  114.7 1.7 %shard_map.123 = (f32[16,32,128]{2,1,0:T(8,128)}, f32[4,40,128]{2,1,0:T(8,128)}) custom-call(f32[16,32,128]{2,1,0:T(8,128)} %all_to_all.39.refs_0_, f32[16,8,128]{2,1,0:T(8,128)} %get-tuple-element.31.refs_1_.refs_2_, f32[8,128]{1,0:T(8,128)} %get-tuple-element.32.refs_2_), custom_call_target="tpu_custom_call" | custom-call | tf_op jit(solution)/shard_map/pallas_call | solution.py:255
  116.4 9.7 %all_to_all.40.refs_0_ = f32[4,40,128]{2,1,0:T(8,128)} all-to-all(f32[4,40,128]{2,1,0:T(8,128)} %get-tuple-element.33), channel_id=1, replica_groups={{0,128,256,384},{8,136,264,392},{16,144,272,400},{24,152,280,408},{32,1..., dimensions={0} | all-to-all | bytes 163840 | tf_op jit(solution)/shard_map/all_to_all | solution.py:268
  126.1 1.8 %shard_map.124 = f32[16,40,128]{2,1,0:T(8,128)} custom-call(f32[4,40,128]{2,1,0:T(8,128)} %all_to_all.40.refs_0_, f32[16,32,128]{2,1,0:T(8,128)} %get-tuple-element.34.refs_1_, f32[16,8,128]{2,1,0:T(8,128)} %get-tuple-element.31.refs_1_.refs_2_, f32[4,40,128]{2,1,0:T(8,128)} %all_to_all.36.refs_0_.refs_3_), custom_call_target="tpu_custom_call" | custom-call | tf_op jit(solution)/shard_map/pallas_call | solution.py:255
  127.9 25.8 %all_to_all.41.end_ref = f32[16,40,128]{2,1,0:T(8,128)} all-to-all(f32[16,40,128]{2,1,0:T(8,128)} %shard_map.124), channel_id=1, replica_groups={{0,8,16,24,32,40,48,56,64,72,80,88,96,104,112,120},{128,136,144,152,160..., dimensions={0} | all-to-all | bytes 655360 | tf_op jit(solution)/shard_map/all_to_all | solution.py:268
  153.7 3.9 %shard_map.125 = (bf16[128,512]{1,0:T(8,128)(2,1)}, bf16[128,512]{1,0:T(8,128)(2,1)}, bf16[128,512]{1,0:T(8,128)(2,1)}, f32[4,128]{1,0:T(4,128)}, f32[8,128]{1,0:T(8,128)}) custom-call(bf16[128,512]{1,0:T(8,128)(2,1)} %q_ref.5, bf16[128,512]{1,0:T(8,128)(2,1)} %k_ref.5, bf16[128,512]{1,0:T(8,128)(2,1)} %v_ref.5, f32[4,128]{1,0:T(4,128)} %decay_ref.7, ...), custom_call_target="tpu_custom_call" | custom-call | tf_op jit(solution)/shard_map/pallas_call | solution.py:255
  157.6 1.3 slice_bitcast_fusion

commit v2 on v1

v2 whole, which is shorter than its diff:
```python
import jax
import jax.numpy as jnp
from jax import lax
from jax.experimental import pallas as pl
from jax.experimental.pallas import tpu as pltpu
from jax.sharding import PartitionSpec as P

DK = 128
STEPS = 128
HEADS = 4
TEAM = 16
WIDTH = 4096
EPS = 1e-06
SCALE = DK ** (-0.5)
Z = 16
Y = 4
OWNERS = Z // HEADS
ROWS = DK // OWNERS
PACKED = ROWS + 1
MESSAGE = ROWS + 2
F32 = jnp.float32
BF16 = jnp.bfloat16

NN = (((1,), (0,)), ((), ()))
NT = (((1,), (1,)), ((), ()))
TN = (((0,), (0,)), ((), ()))


def mm(a, b, dims):
    return lax.dot_general(a, b, dims, preferred_element_type=F32)


def exact(a, b, dims):
    return lax.dot_general(
        a, b, dims, precision=lax.Precision.HIGHEST, preferred_element_type=F32
    )


def parts(a):
    high = a.astype(BF16)
    return high, (a - high.astype(F32)).astype(BF16)


def wide_left(a, b, dims):
    high, low = parts(a)
    return mm(high, b, dims) + mm(low, b, dims)


def wide_right(a, b, dims):
    high, low = parts(b)
    return mm(a, high, dims) + mm(a, low, dims)


def wide_both(a, b, dims):
    ah, al = parts(a)
    bh, bl = parts(b)
    return mm(ah, bh, dims) + (mm(ah, bl, dims) + mm(al, bh, dims))


def grid_index():
    rows = lax.broadcasted_iota(jnp.int32, (STEPS, STEPS), 0)
    cols = lax.broadcasted_iota(jnp.int32, (STEPS, STEPS), 1)
    return rows, cols


def head(ref, h):
    return ref[:, h * DK : (h + 1) * DK]


def slot(h, j):
    return (h * OWNERS + j) * PACKED


def spread_out(out_ref, h, state, row):
    for j in range(OWNERS):
        at = slot(h, j)
        out_ref[at : at + ROWS, :] = state[j * ROWS : (j + 1) * ROWS]
        out_ref[at + ROWS : at + PACKED, :] = row


def state_kernel(k_hbm, v_hbm, decay_hbm, out_hbm, k_ref, v_ref, decay_ref, out_ref, sems):
    loads = [
        pltpu.make_async_copy(source, target, sems.at[i])
        for i, (source, target) in enumerate(
            ((decay_hbm, decay_ref), (k_hbm, k_ref), (v_hbm, v_ref))
        )
    ]
    for load in loads:
        load.start()
    loads[0].wait()
    rows, cols = grid_index()
    decay = decay_ref[...]
    tail = jnp.exp(exact((cols > rows).astype(F32), decay, NT))
    factor = jnp.exp(jnp.sum(decay, axis=1, keepdims=True))
    loads[1].wait()
    loads[2].wait()
    stores = []
    for h in range(HEADS):
        k = head(k_ref, h).astype(F32) * tail[:, h : h + 1]
        state = wide_left(k, head(v_ref, h), TN)
        spread_out(out_ref, h, state, jnp.broadcast_to(factor[h : h + 1], (1, DK)))
        if h % 2:
            span = pl.ds(slot(h - 1, 0), 2 * OWNERS * PACKED)
            store = pltpu.make_async_copy(out_ref.at[span], out_hbm.at[span], sems.at[3 + h // 2])
            store.start()
            stores.append(store)
    for store in stores:
        store.wait()


def row_scan_kernel(in_ref, local_ref, factor_ref, reach_ref, row_ref):
    running = jnp.zeros((ROWS, DK), F32)
    product = jnp.ones((1, DK), F32)
    for z in range(Z):
        at = z * PACKED
        local_ref[z * ROWS : (z + 1) * ROWS, :] = running
        reach_ref[z : z + 1, :] = product
        factor = in_ref[at + ROWS : at + PACKED, :]
        factor_ref[z : z + 1, :] = factor
        running = factor * running + in_ref[at : at + ROWS, :]
        product = factor * product
    for y in range(Y):
        row_ref[y * MESSAGE : y * MESSAGE + ROWS, :] = running
        row_ref[y * MESSAGE + ROWS : (y + 1) * MESSAGE, :] = jnp.broadcast_to(product, (2, DK))


def join_kernel(rows_ref, local_ref, reach_ref, out_ref):
    mine = lax.axis_index("tm") // Z
    running = jnp.zeros((ROWS, DK), F32)
    for y in range(Y - 1):
        at = y * MESSAGE
        longer = rows_ref[at + ROWS : at + PACKED, :] * running + rows_ref[at : at + ROWS, :]
        running = jnp.where(y < mine, longer, running)
    for z in range(Z):
        span = slice(z * ROWS, (z + 1) * ROWS)
        out_ref[span, :] = local_ref[span, :] + reach_ref[z : z + 1, :] * running


def row_scan_back_kernel(in_ref, factor_ref, local_ref, row_ref):
    running = jnp.zeros((ROWS, DK), F32)
    gain = jnp.zeros((1, DK), F32)
    for z in range(Z - 1, -1, -1):
        at = z * PACKED
        local_ref[z * ROWS : (z + 1) * ROWS, :] = running
        running = factor_ref[z : z + 1, :] * running + in_ref[at : at + ROWS, :]
        gain = gain + in_ref[at + ROWS : at + PACKED, :]
    for y in range(Y):
        row_ref[y * MESSAGE : y * MESSAGE + ROWS, :] = running
        row_ref[y * MESSAGE + ROWS : (y + 1) * MESSAGE, :] = jnp.broadcast_to(gain, (2, DK))


def join_back_kernel(rows_ref, local_ref, factor_ref, totals_ref, out_ref):
    mine = lax.axis_index("tm") // Z
    running = jnp.zeros((ROWS, DK), F32)
    for y in range(Y - 1, 0, -1):
        at = y * MESSAGE
        longer = totals_ref[at + ROWS : at + PACKED, :] * running + rows_ref[at : at + ROWS, :]
        running = jnp.where(y > mine, longer, running)
    gain = rows_ref[ROWS:PACKED, :]
    for y in range(1, Y):
        gain = gain + rows_ref[y * MESSAGE + ROWS : y * MESSAGE + PACKED, :]
    product = jnp.ones((1, DK), F32)
    for z in range(Z - 1, -1, -1):
        at = z * PACKED
        out_ref[at : at + ROWS, :] = local_ref[z * ROWS : (z + 1) * ROWS, :] + product * running
        out_ref[at + ROWS : at + PACKED, :] = gain
        product = product * factor_ref[z : z + 1, :]


def decays(decay):
    rows, cols = grid_index()
    lower = (cols <= rows).astype(F32)
    column = exact(lower, decay, NT)
    row = exact(decay, lower, NT)
    return column, row


def weights_of(column, row, visible, h):
    spread = column[:, h : h + 1] - row[h : h + 1, :]
    return jnp.where(visible, jnp.exp(jnp.where(visible, spread, 0.0)), 0.0)


def visible_of(ids_ref):
    rows, cols = grid_index()
    team = jnp.broadcast_to((ids_ref[...] // TEAM).astype(F32), (STEPS, STEPS))
    return (cols <= rows) & (team == team.T)


def packed_state(ref, h):
    starts = [slot(h, j) for j in range(OWNERS)]
    return jnp.concatenate([ref[at : at + ROWS, :] for at in starts], axis=0)


def local_kernel(
    q_ref, k_ref, v_ref, decay_ref, ids_ref, gain_ref, grad_ref,
    scores_ref, weights_ref, out_ref, pull_ref, scales_ref, factor_ref,
):
    decay = decay_ref[...]
    column, row = decays(decay)
    rows, cols = grid_index()
    visible = visible_of(ids_ref)
    scales_ref[...] = jnp.zeros((STEPS, DK), F32)
    scales_ref[:, 0:HEADS] = jnp.exp(column) * SCALE
    scales_ref[:, HEADS : 2 * HEADS] = jnp.exp(exact((cols > rows).astype(F32), decay, NT))
    factor_ref[...] = jnp.broadcast_to(jnp.exp(jnp.sum(decay, axis=1, keepdims=True)), (HEADS, DK))
    for h in range(HEADS):
        span = slice(h * DK, (h + 1) * DK)
        weights = weights_of(column, row, visible, h) * SCALE
        scores = mm(head(q_ref, h), head(k_ref, h), NT) * weights
        weights_ref[:, span] = weights
        scores_ref[:, span] = scores
        out_ref[:, span] = wide_left(scores, head(v_ref, h), NN)
        pull_ref[:, span] = head(grad_ref, h).astype(F32) * head(gain_ref, h)


def grown_of(scales_ref, h):
    return scales_ref[:, h : h + 1]


def tail_of(scales_ref, h):
    return scales_ref[:, HEADS + h : HEADS + h + 1]


def output_kernel(q_ref, scales_ref, pull_ref, near_ref, state_ref, out_ref, sums_ref):
    squares = jnp.zeros((STEPS, DK), F32)
    inners = jnp.zeros((STEPS, DK), F32)
    for h in range(HEADS):
        span = slice(h * DK, (h + 1) * DK)
        inter = wide_right(head(q_ref, h), state_ref[span, :], NN)
        out = head(near_ref, h) + grown_of(scales_ref, h) * inter
        out_ref[:, span] = out
        squares = squares + out * out
        inners = inners + head(pull_ref, h) * out
    ones = jnp.ones((8, DK), F32)
    both = jnp.where(
        lax.broadcasted_iota(jnp.int32, (8, STEPS), 0) == 0,
        exact(ones, squares, NT),
        exact(ones, inners, NT),
    )
    for p in range(8):
        sums_ref[p] = both


def norm_kernel(sums_ref, o_ref, q_ref, scales_ref, pull_ref, grad_ref, adjoint_ref, inverse_ref, own_ref):
    total = sums_ref[0]
    for p in range(1, 8):
        total = total + sums_ref[p]
    inverse = 1.0 / jnp.sqrt(total[0:1] / WIDTH + EPS)
    back = total[1:2] * (inverse * inverse * inverse) / WIDTH
    both = jnp.concatenate([inverse, back, jnp.zeros((6, STEPS), F32)], axis=0).T
    inverse, back = both[:, 0:1], both[:, 1:2]
    inverse_ref[...] = jnp.broadcast_to(inverse, (STEPS, DK))
    for h in range(HEADS):
        out = head(o_ref, h)
        part = jnp.sum(head(grad_ref, h).astype(F32) * (out * inverse), axis=0, keepdims=True)
        adjoint = head(pull_ref, h) * inverse - out * back
        adjoint_ref[:, h * DK : (h + 1) * DK] = adjoint
        own = wide_right(head(q_ref, h), adjoint * grown_of(scales_ref, h), TN)
        spread_out(own_ref, h, own, part)


def local_back_kernel(
    q_ref, k_ref, v_ref, scales_ref, gain_ref, scores_ref, weights_ref, o_ref, inverse_ref, state_ref, adjoint_ref,
    result_ref, dq_ref, dk_ref, dv_ref, dd_ref,
):
    rows, cols = grid_index()
    until = (rows >= cols).astype(F32)
    inverse = inverse_ref[...]
    for h in range(HEADS):
        span = slice(h * DK, (h + 1) * DK)
        q, k, v = head(q_ref, h), head(k_ref, h), head(v_ref, h)
        result_ref[:, span] = (head(o_ref, h) * inverse * head(gain_ref, h)).astype(BF16)
        adjoint = head(adjoint_ref, h)
        scores = head(scores_ref, h)
        slopes = wide_left(adjoint, v, NT)
        joint = scores * slopes
        slopes = slopes * head(weights_ref, h)
        inter = wide_both(adjoint, state_ref[span, :], NT) * grown_of(scales_ref, h)
        dq_ref[:, span] = (wide_left(slopes, k, NN) + inter).astype(BF16)
        dk_ref[:, span] = wide_left(slopes, q, TN)
        dv_ref[:, span] = wide_both(scores, adjoint, TN)
        late = jnp.sum(joint + inter * q.astype(F32), axis=1, keepdims=True)
        columns = jnp.sum(joint, axis=0, keepdims=True)
        dd_ref[h : h + 1, :] = (
            jnp.sum(late * until, axis=0, keepdims=True)
            - exact(jnp.broadcast_to(columns, (8, STEPS)), until, NN)[0:1]
        )


def final_kernel(
    k_ref, v_ref, scales_ref, factor_ref, state_ref, near_dk_ref, near_dv_ref, near_dd_ref, end_ref,
    dk_ref, dv_ref, dd_ref, dg_ref,
):
    rows, cols = grid_index()
    before = (rows < cols).astype(F32)
    for h in range(HEADS):
        span = slice(h * DK, (h + 1) * DK)
        k, v = head(k_ref, h), head(v_ref, h)
        end = packed_state(end_ref, h)
        dk_end = wide_right(v, end, NT) * tail_of(scales_ref, h)
        dk_ref[:, span] = (head(near_dk_ref, h) + dk_end).astype(BF16)
        dv_end = wide_right(k, end, NN) * tail_of(scales_ref, h)
        dv_ref[:, span] = (head(near_dv_ref, h) + dv_end).astype(BF16)
        early = jnp.sum(dk_end * k.astype(F32), axis=1, keepdims=True)
        through = factor_ref[h : h + 1, :] * jnp.sum(end * state_ref[span, :])
        dd_ref[h : h + 1, :] = near_dd_ref[h : h + 1, :] + jnp.sum(early * before, axis=0, keepdims=True) + through
        dg_ref[:, span] = end_ref[slot(h, 0) + ROWS : slot(h, 0) + PACKED, :]


VMEM = pl.BlockSpec(memory_space=pltpu.VMEM)


def call(kernel, shapes, *arrays, specs=None, outs=None, scratch=(), cost=None, limit=16):
    return pl.pallas_call(
        kernel,
        out_shape=[jax.ShapeDtypeStruct(s, d) for s, d in shapes],
        in_specs=specs or [VMEM] * len(arrays),
        out_specs=outs or [VMEM] * len(shapes),
        scratch_shapes=list(scratch),
        cost_estimate=cost,
        compiler_params=pltpu.CompilerParams(vmem_limit_bytes=limit * 1024 * 1024),
    )(*arrays)


Z_GROUPS = [[y * Z + z for z in range(Z)] for y in range(Y)]
Y_GROUPS = [[y * Z + z for y in range(Y)] for z in range(Z)]


def exchange(value, groups, rows):
    peers = value.shape[0] // rows
    moved = lax.all_to_all(
        value.reshape(peers, rows, 1, DK), "tm", 0, 0, axis_index_groups=groups, tiled=True
    )
    return moved.reshape(value.shape)


def after(value, *others):
    return lax.optimization_barrier((value, *others))[0]


def body(queries, keys, values, log_decay, agent_ids, norm_gain, out_grad):
    ids = agent_ids.reshape(1, STEPS)
    gain = norm_gain.reshape(1, HEADS * DK)
    wide = (STEPS, HEADS * DK)
    plain, packed, totals = (Z * ROWS, DK), (Z * PACKED, DK), (Y * MESSAGE, DK)
    few = (Z, DK)
    long_cost = pl.CostEstimate(flops=40_000_000, bytes_accessed=2_000_000, transcendentals=65536)
    hbm = pl.BlockSpec(memory_space=pl.ANY)
    (ends,) = call(
        state_kernel, [(packed, F32)], keys, values, log_decay,
        specs=[hbm] * 3,
        outs=[hbm],
        scratch=[
            pltpu.VMEM(wide, BF16),
            pltpu.VMEM(wide, BF16),
            pltpu.VMEM((HEADS, STEPS), F32),
            pltpu.VMEM(packed, F32),
            pltpu.SemaphoreType.DMA((5,)),
        ],
        limit=60,
    )
    scores, weights, near, pull, scales, factor = call(
        local_kernel,
        [(wide, F32)] * 4 + [((STEPS, DK), F32), ((HEADS, DK), F32)],
        queries, keys, values, log_decay, ids, gain, out_grad,
        cost=long_cost,
    )
    ends = exchange(ends, Z_GROUPS, PACKED)
    local, factors, reach, row = call(
        row_scan_kernel, [(plain, F32), (few, F32), (few, F32), (totals, F32)], ends
    )
    rows = exchange(after(row, near), Y_GROUPS, MESSAGE)
    (entering,) = call(join_kernel, [(plain, F32)], rows, local, reach)
    state = exchange(entering, Z_GROUPS, ROWS)
    out, sums = call(
        output_kernel,
        [(wide, F32), ((8, 8, STEPS), F32)],
        queries, scales, pull, near, state,
    )
    sums = lax.all_to_all(sums, "head", 0, 0, tiled=True)
    adjoint, inverse, own = call(
        norm_kernel,
        [(wide, F32), ((STEPS, DK), F32), (packed, F32)],
        sums, out, queries, scales, pull, out_grad,
    )
    result, query_grad, near_dk, near_dv, near_dd = call(
        local_back_kernel,
        [(wide, BF16), (wide, BF16), (wide, F32), (wide, F32), ((HEADS, STEPS), F32)],
        queries, keys, values, scales, gain, scores, weights, out, inverse, state, adjoint,
        cost=long_cost,
    )
    own = exchange(own, Z_GROUPS, PACKED)
    local, row = call(row_scan_back_kernel, [(plain, F32), (totals, F32)], own, factors)
    row = exchange(row, Y_GROUPS, MESSAGE)
    (leaving,) = call(join_back_kernel, [(packed, F32)], row, local, factors, rows)
    end = exchange(leaving, Z_GROUPS, PACKED)
    key_grad, value_grad, decay_grad, gain_grad = call(
        final_kernel,
        [(wide, BF16), (wide, BF16), ((HEADS, STEPS), F32), ((1, HEADS * DK), F32)],
        keys, values, scales, factor, state, near_dk, near_dv, near_dd, end,
    )
    return result, query_grad, key_grad, value_grad, decay_grad, gain_grad.reshape(-1)


def solution(mesh):
    wide = P("tm", "head")
    return jax.shard_map(
        body,
        mesh=mesh,
        in_specs=(wide, wide, wide, P("head", "tm"), P("tm"), P("head"), wide),
        out_specs=(wide, wide, wide, wide, P("head", "tm"), P("head")),
        check_vma=False,
    )
```

time: 160 us -> 138 us (0.86)
  blocking collectives: 138 us -> 74.1 us
  waiting for transfers between devices: 0 us -> 32.7 us
  starting transfers between devices: 0 us -> 21.9 us
  Pallas kernels: 18.7 us -> 7.8 us
    all_to_all x7 -> x5, blocking collectives: 138 us -> 74.1 us  [the longest x4 64.6 us: exchange(): lax.all_to_all(value.reshape(peers, rows, 1, DK), 'tm', 0, 0, axis_index_...]
    all_to_all x0 -> x2, waiting for transfers between devices: none -> 32.7 us  [exchange(): lax.all_to_all(value.reshape(peers, rows, 1, DK), 'tm', 0, 0, axis_index_...]
    all_to_all x0 -> x2, starting transfers between devices: none -> 21.9 us  [exchange(): lax.all_to_all(value.reshape(peers, rows, 1, DK), 'tm', 0, 0, axis_index_...]
    pallas_call x8 -> x10, Pallas kernels: 18.7 us -> 7.8 us  [call(): pl.pallas_call(kernel, out_shape=[jax.ShapeDtypeStruct(s, d) for s, d in...]
  transfers between devices with their start and end apart: 0 -> 2, of which waited for: 0 -> 2; matrix products, arithmetic and copies ran while one was open for 0% -> 0% of each run, Pallas kernels for 0% -> 2%
where the time goes in v2:
time: 138 us
  blocking collectives  74.1 us (54%)
  waiting for transfers between devices  32.7 us (24%)
  starting transfers between devices  21.9 us (16%)
  Pallas kernels  7.8 us (6%)
    all_to_all x4, blocking collectives, exchange(): lax.all_to_all(value.reshape(peers, rows, 1, DK), 'tm', 0, 0, axis_index_...  64.6 us
    all_to_all x2, waiting for transfers between devices, exchange(): lax.all_to_all(value.reshape(peers, rows, 1, DK), 'tm', 0, 0, axis_index_...  32.7 us
    all_to_all x2, starting transfers between devices, exchange(): lax.all_to_all(value.reshape(peers, rows, 1, DK), 'tm', 0, 0, axis_index_...  21.9 us
    all_to_all x1, blocking collectives, body(): sums = lax.all_to_all(sums, 'head', 0, 0, tiled=True)  9.55 us
    pallas_call x10, Pallas kernels, call(): pl.pallas_call(kernel, out_shape=[jax.ShapeDtypeStruct(s, d) for s, d in...  7.8 us
  transfers between devices with their start and end apart: 2, of which 2 were waited for; matrix products, arithmetic and copies ran while one was open for 0% of the time, Pallas kernels for 2%

profile of v2, /device:TPU:32, one launch (start us, length us, event | category | flops | bytes accessed | tf_op | source)
XLA Modules:
  0.0 137.9 jit_solution(295262512703219257)
XLA Ops:
  0.6 2.1 %shard_map.119 = f32[528,128]{1,0:T(8,128)} custom-call(bf16[128,512]{1,0:T(8,128)(2,1)} %k_ref.5, bf16[128,512]{1,0:T(8,128)(2,1)} %v_ref.5, f32[4,128]{1,0:T(4,128)} %decay_hbm.1), custom_call_target="tpu_custom_call" | custom-call | tf_op jit(solution)/shard_map/pallas_call | solution.py:314
  2.7 0.0 copy-start
  2.7 0.0 copy-start.1
  2.7 0.0 copy-start.2
  2.7 0.0 copy-start.3
  2.8 0.0 copy-start.5
  2.8 15.4 %all-to-all-start = ((f32[16,33,1,128]{3,2,1,0:T(1,128)}), f32[16,33,1,128]{3,2,1,0:T(1,128)S(1)}, u32[]{:S(2)}, u32[]{:S(2)}) async-start(f32[16,33,1,128]{3,2,1,0:T(1,128)} %bitcast.33), calls=%async_computation | async-start | bytes 540672 | tf_op jit(solution)/shard_map/all_to_all | solution.py:331
  18.1 0.0 copy-start.6
  18.2 0.6 copy-done.4
  18.8 0.0 copy-done.6
  18.8 0.6 shard_map.118
  19.4 16.7 %all-to-all-done = f32[16,33,1,128]{3,2,1,0:T(1,128)S(1)} async-done(((f32[16,33,1,128]{3,2,1,0:T(1,128)}), f32[16,33,1,128]{3,2,1,0:T(1,128)S(1)}, u32[]{:S(2)}, u32[]{:S(2)}) %all-to-all-start) | async-done | bytes 270368 | tf_op jit(solution)/shard_map/all_to_all | solution.py:331
  36.2 9.9 %all_to_all.35 = f32[4,34,1,128]{3,2,1,0:T(1,128)S(1)} all-to-all(f32[4,34,1,128]{3,2,1,0:T(1,128)S(1)} %bitcast.28), channel_id=1, replica_groups={{0,128,256,384},{8,136,264,392},{16,144,272,400},{24,152,280,408},{32,1..., dimensions={0} | all-to-all | bytes 139264 | tf_op jit(solution)/shard_map/all_to_all | solution.py:331
  46.1 24.0 %all_to_all.36 = f32[16,32,1,128]{3,1,2,0:T(8,128)S(1)} all-to-all(f32[16,32,1,128]{3,1,2,0:T(8,128)S(1)} %bitcast.23), channel_id=1, replica_groups={{0,8,16,24,32,40,48,56,64,72,80,88,96,104,112,120},{128,136,144,152,160..., dimensions={0} | all-to-all | bytes 524288 | tf_op jit(solution)/shard_map/all_to_all | solution.py:331
  70.1 0.5 shard_map.122
  70.6 9.5 %all_to_all.37.sums_ref = f32[8,8,128]{2,1,0:T(8,128)S(1)} all-to-all(f32[8,8,128]{2,1,0:T(8,128)S(1)} %get-tuple-element.43), channel_id=1, replica_groups=mesh['tm'=64,'head'=8] {'head'}, dimensions={0} | all-to-all | bytes 65536 | tf_op jit(solution)/shard_map/all_to_all | solution.py:380
  80.2 0.5 shard_map.123
  80.7 22.7 %all_to_all.38 = f32[16,33,1,128]{3,2,1,0:T(1,128)S(1)} all-to-all(f32[16,33,1,128]{3,2,1,0:T(1,128)S(1)} %bitcast.27), channel_id=1, replica_groups={{0,8,16,24,32,40,48,56,64,72,80,88,96,104,112,120},{128,136,144,152,160..., dimensions={0} | all-to-all | bytes 540672 | tf_op jit(solution)/shard_map/all_to_all | solution.py:331
  103.4 8.0 %all_to_all.39 = f32[4,34,1,128]{3,2,1,0:T(1,128)S(1)} all-to-all(f32[4,34,1,128]{3,2,1,0:T(1,128)S(1)} %bitcast.29), channel_id=1, replica_groups={{0,128,256,384},{8,136,264,392},{16,144,272,400},{24,152,280,408},{32,1..., dimensions={0} | all-to-all | bytes 139264 | tf_op jit(solution)/shard_map/all_to_all | solution.py:331
  111.5 0.7 shard_map.126
  112.2 6.6 %all-to-all-start.6 = ((f32[16,33,1,128]{3,2,1,0:T(1,128)}), f32[16,33,1,128]{3,2,1,0:T(1,128)S(1)}, u32[]{:S(2)}, u32[]{:S(2)}) async-start(f32[16,33,1,128]{3,2,1,0:T(1,128)} %bitcast.13), calls=%async_computation.6 | async-start | bytes 540672 | tf_op jit(solution)/shard_map/all_to_all | solution.py:331
  118.7 2.0 %shard_map.124 = (bf16[128,512]{1,0:T(8,128)(2,1)}, bf16[128,512]{1,0:T(8,128)(2,1)}, f32[128,512]{1,0:T(8,128)S(1)}, f32[128,512]{1,0:T(8,128)S(1)}, f32[4,128]{1,0:T(4,128)S(1)}) custom-call(bf16[128,512]{1,0:T(8,128)(2,1)S(1)} %copy-done, bf16[128,512]{1,0:T(8,128)(2,1)S(1)} %copy-done.1, bf16[128,512]{1,0:T(8,128)(2,1)S(1)} %copy-done.2, ...), custom_call_target="tpu_custom_call" | custom-call | flops 40000000 | bytes 2000000 | tf_op jit(solution)/shard_map/pallas_call | solution.py:314
  120.8 16.0 %all-to-all-done.6 = f32[16,33,1,128]{3,2,1,0:T(1,128)S(1)} async-done(((f32[16,33,1,128]{3,2,1,0:T(1,128)}), f32[16,33,1,128]{3,2,1,0:T(1,128)S(1)}, u32[]{:S(2)}, u32[]{:S(2)}) %all-to-all-start.6) | async-done | bytes 270368 | tf_op jit(solution)/shard_map/all_to_all | solution.py:331
  136.7 1.1 shard_map.127
  (9 shorter events, 0.1 us)
Async XLA Ops:
  2.7 15.4 %copy-start = (bf16[128,512]{1,0:T(8,128)(2,1)S(1)}, bf16[128,512]{1,0:T(8,128)(2,1)}, u32[]{:S(2)}) copy-start(bf16[128,512]{1,0:T(8,128)(2,1)} %q_ref.7) | copy-start | bytes 393220
  2.7 15.4 %copy-start.1 = (bf16[128,512]{1,0:T(8,128)(2,1)S(1)}, bf16[128,512]{1,0:T(8,128)(2,1)}, u32[]{:S(2)}) copy-start(bf16[128,512]{1,0:T(8,128)(2,1)} %k_ref.5) | copy-start | bytes 393220
  2.7 15.4 %copy-start.2 = (bf16[128,512]{1,0:T(8,128)(2,1)S(1)}, bf16[128,512]{1,0:T(8,128)(2,1)}, u32[]{:S(2)}) copy-start(bf16[128,512]{1,0:T(8,128)(2,1)} %v_ref.5) | copy-start | bytes 393220
  2.7 15.4 %copy-start.3 = (bf16[128,512]{1,0:T(8,128)(2,1)S(1)}, bf16[128,512]{1,0:T(8,128)(2,1)}, u32[]{:S(2)}) copy-start(bf16[128,512]{1,0:T(8,128)(2,1)} %grad_ref.3) | copy-start | bytes 393220
  2.8 15.4 %copy-start.5 = (f32[512]{0:T(512)S(1)}, f32[512]{0:T(512)}, u32[]{:S(2)}) copy-start(f32[512]{0:T(512)} %param.12) | copy-start | bytes 6148
  2.8 33.4 %all-to-all-start = ((f32[16,33,1,128]{3,2,1,0:T(1,128)}), f32[16,33,1,128]{3,2,1,0:T(1,128)S(1)}, u32[]{:S(2)}, u32[]{:S(2)}) async-start(f32[16,33,1,128]{3,2,1,0:T(1,128)} %bitcast.33), calls=%async_computation | async-start | bytes 540672 | tf_op jit(solution)/shard_map/all_to_all | solution.py:331
  18.1 0.7 copy-start.4
  18.1 0.7 copy-start.6
  112.2 24.5 %all-to-all-start.6 = ((f32[16,33,1,128]{3,2,1,0:T(1,128)}), f32[16,33,1,128]{3,2,1,0:T(1,128)S(1)}, u32[]{:S(2)}, u32[]{:S(2)}) async-start(f32[16,33,1,128]{3,2,1,0:T(1,128)} %bitcast.13), calls=%async_computation.6 | async-start | bytes 540672 | tf_op jit(solution)/shard_map/all_to_all | solution.py:331

commit v3 on v2

--- a/solution.py
+++ b/solution.py
@@ -11,6 +11,8 @@
 TEAM = 16
 WIDTH = 4096
 EPS = 1e-06
+CORES = 2
+STAGGER_NS = 4000
 SCALE = DK ** (-0.5)
 Z = 16
 Y = 4
@@ -88,6 +90,10 @@
     for load in loads:
         load.start()
     loads[0].wait()
+    @pl.when(lax.axis_index("head") % CORES == 0)
+    def _wait():
+        pl.delay(STAGGER_NS)
+
     rows, cols = grid_index()
     decay = decay_ref[...]
     tail = jnp.exp(exact((cols > rows).astype(F32), decay, NT))
@@ -242,6 +248,10 @@
 
 
 def norm_kernel(sums_ref, o_ref, q_ref, scales_ref, pull_ref, grad_ref, adjoint_ref, inverse_ref, own_ref):
+    @pl.when(lax.axis_index("head") % CORES == 0)
+    def _wait():
+        pl.delay(STAGGER_NS)
+
     total = sums_ref[0]
     for p in range(1, 8):
         total = total + sums_ref[p]

time: 138 us -> 133 us (0.964)
  the two profiles are of different devices: /device:TPU:32 before, /device:TPU:2 now
where the time goes in v3:
time: 133 us; the launch traced here: 132 us
  blocking collectives  67 us (50%)
  waiting for transfers between devices  28.6 us (22%)
  starting transfers between devices  19.5 us (15%)
  Pallas kernels  15.7 us (12%)
    all_to_all x4, blocking collectives, exchange(): lax.all_to_all(value.reshape(peers, rows, 1, DK), 'tm', 0, 0, axis_index_...  58.4 us
    all_to_all x2, waiting for transfers between devices, exchange(): lax.all_to_all(value.reshape(peers, rows, 1, DK), 'tm', 0, 0, axis_index_...  28.6 us
    all_to_all x2, starting transfers between devices, exchange(): lax.all_to_all(value.reshape(peers, rows, 1, DK), 'tm', 0, 0, axis_index_...  19.5 us
    pallas_call x10, Pallas kernels, call(): pl.pallas_call(kernel, out_shape=[jax.ShapeDtypeStruct(s, d) for s, d in...  15.7 us
    all_to_all x1, blocking collectives, body(): sums = lax.all_to_all(sums, 'head', 0, 0, tiled=True)  8.62 us
  transfers between devices with their start and end apart: 2, of which 2 were waited for; matrix products, arithmetic and copies ran while one was open for 0% of the time, Pallas kernels for 2%

profile of v3, /device:TPU:2, one launch (start us, length us, event | category | flops | bytes accessed | tf_op | source)
XLA Modules:
  0.0 132.3 jit_solution(17314479773220548340)
XLA Ops:
  0.6 6.0 %shard_map.119 = f32[528,128]{1,0:T(8,128)} custom-call(bf16[128,512]{1,0:T(8,128)(2,1)} %k_ref.5, bf16[128,512]{1,0:T(8,128)(2,1)} %v_ref.5, f32[4,128]{1,0:T(4,128)} %decay_hbm.1), custom_call_target="tpu_custom_call" | custom-call | tf_op jit(solution)/shard_map/pallas_call | solution.py:324
  6.6 0.0 copy-start
  6.6 0.0 copy-start.1
  6.7 0.0 copy-start.2
  6.7 0.0 copy-start.3
  6.7 0.0 copy-start.5
  6.7 15.3 %all-to-all-start = ((f32[16,33,1,128]{3,2,1,0:T(1,128)}), f32[16,33,1,128]{3,2,1,0:T(1,128)S(1)}, u32[]{:S(2)}, u32[]{:S(2)}) async-start(f32[16,33,1,128]{3,2,1,0:T(1,128)} %bitcast.33), calls=%async_computation | async-start | bytes 540672 | tf_op jit(solution)/shard_map/all_to_all | solution.py:341
  22.0 0.0 copy-start.4
  22.1 0.0 copy-start.6
  22.1 0.6 copy-done.4
  22.7 0.6 shard_map.118
  23.3 14.6 %all-to-all-done = f32[16,33,1,128]{3,2,1,0:T(1,128)S(1)} async-done(((f32[16,33,1,128]{3,2,1,0:T(1,128)}), f32[16,33,1,128]{3,2,1,0:T(1,128)S(1)}, u32[]{:S(2)}, u32[]{:S(2)}) %all-to-all-start) | async-done | bytes 270368 | tf_op jit(solution)/shard_map/all_to_all | solution.py:341
  38.0 9.9 %all_to_all.35 = f32[4,34,1,128]{3,2,1,0:T(1,128)S(1)} all-to-all(f32[4,34,1,128]{3,2,1,0:T(1,128)S(1)} %bitcast.28), channel_id=1, replica_groups={{0,128,256,384},{8,136,264,392},{16,144,272,400},{24,152,280,408},{32,1..., dimensions={0} | all-to-all | bytes 139264 | tf_op jit(solution)/shard_map/all_to_all | solution.py:341
  48.0 18.8 %all_to_all.36 = f32[16,32,1,128]{3,1,2,0:T(8,128)S(1)} all-to-all(f32[16,32,1,128]{3,1,2,0:T(8,128)S(1)} %bitcast.23), channel_id=1, replica_groups={{0,8,16,24,32,40,48,56,64,72,80,88,96,104,112,120},{128,136,144,152,160..., dimensions={0} | all-to-all | bytes 524288 | tf_op jit(solution)/shard_map/all_to_all | solution.py:341
  66.8 0.5 shard_map.122
  67.3 8.6 %all_to_all.37.sums_ref = f32[8,8,128]{2,1,0:T(8,128)S(1)} all-to-all(f32[8,8,128]{2,1,0:T(8,128)S(1)} %get-tuple-element.43), channel_id=1, replica_groups=mesh['tm'=64,'head'=8] {'head'}, dimensions={0} | all-to-all | bytes 65536 | tf_op jit(solution)/shard_map/all_to_all | solution.py:390
  76.0 4.5 %shard_map.123 = (f32[128,512]{1,0:T(8,128)S(1)}, f32[128,128]{1,0:T(8,128)S(1)}, f32[528,128]{1,0:T(8,128)S(1)}) custom-call(f32[8,8,128]{2,1,0:T(8,128)S(1)} %all_to_all.37.sums_ref, f32[128,512]{1,0:T(8,128)S(1)} %get-tuple-element.42.o_ref, bf16[128,512]{1,0:T(8,128)(2,1)S(1)} %copy-done, f32[128,128]{1,0:T(8,128)S(1)} %get-tuple-element.33.scales_ref, ...), custom_call_target="tpu_custom_call" | custom-call | tf_op jit(solution)/shard_map/pallas_call | solution.py:324
  80.5 21.7 %all_to_all.38 = f32[16,33,1,128]{3,2,1,0:T(1,128)S(1)} all-to-all(f32[16,33,1,128]{3,2,1,0:T(1,128)S(1)} %bitcast.27), channel_id=1, replica_groups={{0,8,16,24,32,40,48,56,64,72,80,88,96,104,112,120},{128,136,144,152,160..., dimensions={0} | all-to-all | bytes 540672 | tf_op jit(solution)/shard_map/all_to_all | solution.py:341
  102.2 8.0 %all_to_all.39 = f32[4,34,1,128]{3,2,1,0:T(1,128)S(1)} all-to-all(f32[4,34,1,128]{3,2,1,0:T(1,128)S(1)} %bitcast.29), channel_id=1, replica_groups={{0,128,256,384},{8,136,264,392},{16,144,272,400},{24,152,280,408},{32,1..., dimensions={0} | all-to-all | bytes 139264 | tf_op jit(solution)/shard_map/all_to_all | solution.py:341
  110.2 0.7 shard_map.126
  110.9 4.2 %all-to-all-start.6 = ((f32[16,33,1,128]{3,2,1,0:T(1,128)}), f32[16,33,1,128]{3,2,1,0:T(1,128)S(1)}, u32[]{:S(2)}, u32[]{:S(2)}) async-start(f32[16,33,1,128]{3,2,1,0:T(1,128)} %bitcast.13), calls=%async_computation.6 | async-start | bytes 540672 | tf_op jit(solution)/shard_map/all_to_all | solution.py:341
  115.1 2.0 %shard_map.124 = (bf16[128,512]{1,0:T(8,128)(2,1)}, bf16[128,512]{1,0:T(8,128)(2,1)}, f32[128,512]{1,0:T(8,128)S(1)}, f32[128,512]{1,0:T(8,128)S(1)}, f32[4,128]{1,0:T(4,128)S(1)}) custom-call(bf16[128,512]{1,0:T(8,128)(2,1)S(1)} %copy-done, bf16[128,512]{1,0:T(8,128)(2,1)S(1)} %copy-done.1, bf16[128,512]{1,0:T(8,128)(2,1)S(1)} %copy-done.2, ...), custom_call_target="tpu_custom_call" | custom-call | flops 40000000 | bytes 2000000 | tf_op jit(solution)/shard_map/pallas_call | solution.py:324
  117.2 14.0 %all-to-all-done.6 = f32[16,33,1,128]{3,2,1,0:T(1,128)S(1)} async-done(((f32[16,33,1,128]{3,2,1,0:T(1,128)}), f32[16,33,1,128]{3,2,1,0:T(1,128)S(1)}, u32[]{:S(2)}, u32[]{:S(2)}) %all-to-all-start.6) | async-done | bytes 270368 | tf_op jit(solution)/shard_map/all_to_all | solution.py:341
  131.2 1.1 shard_map.127
  (9 shorter events, 0.1 us)
Async XLA Ops:
  6.6 15.4 %copy-start = (bf16[128,512]{1,0:T(8,128)(2,1)S(1)}, bf16[128,512]{1,0:T(8,128)(2,1)}, u32[]{:S(2)}) copy-start(bf16[128,512]{1,0:T(8,128)(2,1)} %q_ref.7) | copy-start | bytes 393220
  6.6 15.4 %copy-start.1 = (bf16[128,512]{1,0:T(8,128)(2,1)S(1)}, bf16[128,512]{1,0:T(8,128)(2,1)}, u32[]{:S(2)}) copy-start(bf16[128,512]{1,0:T(8,128)(2,1)} %k_ref.5) | copy-start | bytes 393220
  6.7 15.4 %copy-start.2 = (bf16[128,512]{1,0:T(8,128)(2,1)S(1)}, bf16[128,512]{1,0:T(8,128)(2,1)}, u32[]{:S(2)}) copy-start(bf16[128,512]{1,0:T(8,128)(2,1)} %v_ref.5) | copy-start | bytes 393220
  6.7 15.4 %copy-start.3 = (bf16[128,512]{1,0:T(8,128)(2,1)S(1)}, bf16[128,512]{1,0:T(8,128)(2,1)}, u32[]{:S(2)}) copy-start(bf16[128,512]{1,0:T(8,128)(2,1)} %grad_ref.3) | copy-start | bytes 393220
  6.7 15.4 %copy-start.5 = (f32[512]{0:T(512)S(1)}, f32[512]{0:T(512)}, u32[]{:S(2)}) copy-start(f32[512]{0:T(512)} %param.12) | copy-start | bytes 6148
  6.7 31.3 %all-to-all-start = ((f32[16,33,1,128]{3,2,1,0:T(1,128)}), f32[16,33,1,128]{3,2,1,0:T(1,128)S(1)}, u32[]{:S(2)}, u32[]{:S(2)}) async-start(f32[16,33,1,128]{3,2,1,0:T(1,128)} %bitcast.33), calls=%async_computation | async-start | bytes 540672 | tf_op jit(solution)/shard_map/all_to_all | solution.py:341
  22.0 0.7 copy-start.4
  22.1 0.7 copy-start.6
  110.9 20.2 %all-to-all-start.6 = ((f32[16,33,1,128]{3,2,1,0:T(1,128)}), f32[16,33,1,128]{3,2,1,0:T(1,128)S(1)}, u32[]{:S(2)}, u32[]{:S(2)}) async-start(f32[16,33,1,128]{3,2,1,0:T(1,128)} %bitcast.13), calls=%async_computation.6 | async-start | bytes 540672 | tf_op jit(solution)/shard_map/all_to_all | solution.py:341

commit v4 on v3

--- a/solution.py
+++ b/solution.py
@@ -12,6 +12,7 @@
 WIDTH = 4096
 EPS = 1e-06
 CORES = 2
+STAGGER_FIRST_NS = 5000
 STAGGER_NS = 4000
 SCALE = DK ** (-0.5)
 Z = 16
@@ -20,6 +21,9 @@
 ROWS = DK // OWNERS
 PACKED = ROWS + 1
 MESSAGE = ROWS + 2
+TIMES = Y * Z
+THIN = HEADS * DK // TIMES
+THICK = THIN + 1
 F32 = jnp.float32
 BF16 = jnp.bfloat16
 
@@ -92,7 +96,7 @@
     loads[0].wait()
     @pl.when(lax.axis_index("head") % CORES == 0)
     def _wait():
-        pl.delay(STAGGER_NS)
+        pl.delay(STAGGER_FIRST_NS)
 
     rows, cols = grid_index()
     decay = decay_ref[...]
@@ -100,46 +104,43 @@
     factor = jnp.exp(jnp.sum(decay, axis=1, keepdims=True))
     loads[1].wait()
     loads[2].wait()
-    stores = []
     for h in range(HEADS):
         k = head(k_ref, h).astype(F32) * tail[:, h : h + 1]
         state = wide_left(k, head(v_ref, h), TN)
-        spread_out(out_ref, h, state, jnp.broadcast_to(factor[h : h + 1], (1, DK)))
-        if h % 2:
-            span = pl.ds(slot(h - 1, 0), 2 * OWNERS * PACKED)
-            store = pltpu.make_async_copy(out_ref.at[span], out_hbm.at[span], sems.at[3 + h // 2])
-            store.start()
-            stores.append(store)
-    for store in stores:
-        store.wait()
-
-
-def row_scan_kernel(in_ref, local_ref, factor_ref, reach_ref, row_ref):
-    running = jnp.zeros((ROWS, DK), F32)
-    product = jnp.ones((1, DK), F32)
-    for z in range(Z):
-        at = z * PACKED
-        local_ref[z * ROWS : (z + 1) * ROWS, :] = running
-        reach_ref[z : z + 1, :] = product
-        factor = in_ref[at + ROWS : at + PACKED, :]
-        factor_ref[z : z + 1, :] = factor
-        running = factor * running + in_ref[at : at + ROWS, :]
-        product = factor * product
-    for y in range(Y):
-        row_ref[y * MESSAGE : y * MESSAGE + ROWS, :] = running
-        row_ref[y * MESSAGE + ROWS : (y + 1) * MESSAGE, :] = jnp.broadcast_to(product, (2, DK))
-
-
-def join_kernel(rows_ref, local_ref, reach_ref, out_ref):
+        row = jnp.broadcast_to(factor[h : h + 1], (1, DK))
+        for j in range(DK // THIN):
+            at = owner(h, j) * THICK
+            out_ref[at : at + THIN, :] = state[j * THIN : (j + 1) * THIN]
+            out_ref[at + THIN : at + THICK, :] = row
+    store = pltpu.make_async_copy(out_ref, out_hbm, sems.at[3])
+    store.start()
+    store.wait()
+
+
+def owner(h, j):
+    return (j // OWNERS) * Z + h * OWNERS + j % OWNERS
+
+
+def scan_kernel(in_ref, out_ref, own_ref, totals_ref, factor_ref):
+    running = jnp.zeros((THIN, DK), F32)
+    totals_ref[...] = jnp.zeros((2 * Y, DK), F32)
+    for t in range(TIMES):
+        at = t * THICK
+        out_ref[t * THIN : (t + 1) * THIN, :] = running
+        factor = in_ref[at + THIN : at + THICK, :]
+        factor_ref[t : t + 1, :] = factor
+        running = factor * running + in_ref[at : at + THIN, :]
+        product = factor if t % Z == 0 else product * factor
+        if t % Z == Z - 1:
+            totals_ref[t // Z : t // Z + 1, :] = product
     mine = lax.axis_index("tm") // Z
-    running = jnp.zeros((ROWS, DK), F32)
-    for y in range(Y - 1):
-        at = y * MESSAGE
-        longer = rows_ref[at + ROWS : at + PACKED, :] * running + rows_ref[at : at + ROWS, :]
-        running = jnp.where(y < mine, longer, running)
-    for z in range(Z):
-        span = slice(z * ROWS, (z + 1) * ROWS)
-        out_ref[span, :] = local_ref[span, :] + reach_ref[z : z + 1, :] * running
+    own_ref[...] = factor_ref[pl.ds(pl.multiple_of(mine * Z, Z), Z), :]
+
+
+def state_of(ref, h):
+    return jnp.concatenate(
+        [ref[owner(h, j) * THIN : (owner(h, j) + 1) * THIN, :] for j in range(DK // THIN)], axis=0
+    )
 
 
 def row_scan_back_kernel(in_ref, factor_ref, local_ref, row_ref):
@@ -160,7 +161,7 @@
     running = jnp.zeros((ROWS, DK), F32)
     for y in range(Y - 1, 0, -1):
         at = y * MESSAGE
-        longer = totals_ref[at + ROWS : at + PACKED, :] * running + rows_ref[at : at + ROWS, :]
+        longer = totals_ref[y : y + 1, :] * running + rows_ref[at : at + ROWS, :]
         running = jnp.where(y > mine, longer, running)
     gain = rows_ref[ROWS:PACKED, :]
     for y in range(1, Y):
@@ -232,7 +233,7 @@
     inners = jnp.zeros((STEPS, DK), F32)
     for h in range(HEADS):
         span = slice(h * DK, (h + 1) * DK)
-        inter = wide_right(head(q_ref, h), state_ref[span, :], NN)
+        inter = wide_right(head(q_ref, h), state_of(state_ref, h), NN)
         out = head(near_ref, h) + grown_of(scales_ref, h) * inter
         out_ref[:, span] = out
         squares = squares + out * out
@@ -285,7 +286,7 @@
         slopes = wide_left(adjoint, v, NT)
         joint = scores * slopes
         slopes = slopes * head(weights_ref, h)
-        inter = wide_both(adjoint, state_ref[span, :], NT) * grown_of(scales_ref, h)
+        inter = wide_both(adjoint, state_of(state_ref, h), NT) * grown_of(scales_ref, h)
         dq_ref[:, span] = (wide_left(slopes, k, NN) + inter).astype(BF16)
         dk_ref[:, span] = wide_left(slopes, q, TN)
         dv_ref[:, span] = wide_both(scores, adjoint, TN)
@@ -312,7 +313,7 @@
         dv_end = wide_right(k, end, NN) * tail_of(scales_ref, h)
         dv_ref[:, span] = (head(near_dv_ref, h) + dv_end).astype(BF16)
         early = jnp.sum(dk_end * k.astype(F32), axis=1, keepdims=True)
-        through = factor_ref[h : h + 1, :] * jnp.sum(end * state_ref[span, :])
+        through = factor_ref[h : h + 1, :] * jnp.sum(end * state_of(state_ref, h))
         dd_ref[h : h + 1, :] = near_dd_ref[h : h + 1, :] + jnp.sum(early * before, axis=0, keepdims=True) + through
         dg_ref[:, span] = end_ref[slot(h, 0) + ROWS : slot(h, 0) + PACKED, :]
 
@@ -354,18 +355,19 @@
     wide = (STEPS, HEADS * DK)
     plain, packed, totals = (Z * ROWS, DK), (Z * PACKED, DK), (Y * MESSAGE, DK)
     few = (Z, DK)
+    thin, thick = (TIMES * THIN, DK), (TIMES * THICK, DK)
     long_cost = pl.CostEstimate(flops=40_000_000, bytes_accessed=2_000_000, transcendentals=65536)
     hbm = pl.BlockSpec(memory_space=pl.ANY)
     (ends,) = call(
-        state_kernel, [(packed, F32)], keys, values, log_decay,
+        state_kernel, [(thick, F32)], keys, values, log_decay,
         specs=[hbm] * 3,
         outs=[hbm],
         scratch=[
             pltpu.VMEM(wide, BF16),
             pltpu.VMEM(wide, BF16),
             pltpu.VMEM((HEADS, STEPS), F32),
-            pltpu.VMEM(packed, F32),
-            pltpu.SemaphoreType.DMA((5,)),
+            pltpu.VMEM(thick, F32),
+            pltpu.SemaphoreType.DMA((4,)),
         ],
         limit=60,
     )
@@ -375,13 +377,14 @@
         queries, keys, values, log_decay, ids, gain, out_grad,
         cost=long_cost,
     )
-    ends = exchange(ends, Z_GROUPS, PACKED)
-    local, factors, reach, row = call(
-        row_scan_kernel, [(plain, F32), (few, F32), (few, F32), (totals, F32)], ends
-    )
-    rows = exchange(after(row, near), Y_GROUPS, MESSAGE)
-    (entering,) = call(join_kernel, [(plain, F32)], rows, local, reach)
-    state = exchange(entering, Z_GROUPS, ROWS)
+    ends = exchange(ends, None, THICK)
+    entering, factors, rows = call(
+        scan_kernel,
+        [(thin, F32), (few, F32), ((2 * Y, DK), F32)],
+        ends,
+        scratch=[pltpu.VMEM((TIMES, DK), F32)],
+    )
+    state = exchange(after(entering, near), None, THIN)
     out, sums = call(
         output_kernel,
         [(wide, F32), ((8, 8, STEPS), F32)],

time: 133 us -> 133 us (level)
  blocking collectives: 67 us -> 60.5 us
  starting transfers between devices: 19.5 us -> 23 us
  waiting for transfers between devices: 28.6 us -> 30.4 us
    all_to_all x4 -> x3, blocking collectives: 58.4 us -> 51.9 us  [exchange(): lax.all_to_all(value.reshape(peers, rows, 1, DK), 'tm', 0, 0, axis_index_...]
    all_to_all x2, starting transfers between devices: 19.5 us -> 23 us  [exchange(): lax.all_to_all(value.reshape(peers, rows, 1, DK), 'tm', 0, 0, axis_index_...]
    all_to_all x2, waiting for transfers between devices: 28.6 us -> 30.4 us  [exchange(): lax.all_to_all(value.reshape(peers, rows, 1, DK), 'tm', 0, 0, axis_index_...]
    pallas_call x10 -> x9, Pallas kernels: 15.7 us -> 16.8 us  [call(): pl.pallas_call(kernel, out_shape=[jax.ShapeDtypeStruct(s, d) for s, d in...]
where the time goes in v4:
time: 133 us; the launch traced here: 132 us
  blocking collectives  60.5 us (45%)
  waiting for transfers between devices  30.4 us (23%)
  starting transfers between devices  23 us (17%)
  Pallas kernels  16.8 us (13%)
    all_to_all x3, blocking collectives, exchange(): lax.all_to_all(value.reshape(peers, rows, 1, DK), 'tm', 0, 0, axis_index_...  51.9 us
    all_to_all x2, waiting for transfers between devices, exchange(): lax.all_to_all(value.reshape(peers, rows, 1, DK), 'tm', 0, 0, axis_index_...  30.4 us
    all_to_all x2, starting transfers between devices, exchange(): lax.all_to_all(value.reshape(peers, rows, 1, DK), 'tm', 0, 0, axis_index_...  23 us
    pallas_call x9, Pallas kernels, call(): pl.pallas_call(kernel, out_shape=[jax.ShapeDtypeStruct(s, d) for s, d in...  16.8 us
    all_to_all x1, blocking collectives, body(): sums = lax.all_to_all(sums, 'head', 0, 0, tiled=True)  8.62 us
  transfers between devices with their start and end apart: 2, of which 2 were waited for; matrix products, arithmetic and copies ran while one was open for 0% of the time, Pallas kernels for 2%

profile of v4, /device:TPU:2, one launch (start us, length us, event | category | flops | bytes accessed | tf_op | source)
XLA Modules:
  0.0 132.1 jit_solution(12059417310458742057)
XLA Ops:
  0.6 7.0 %shard_map.119 = f32[576,128]{1,0:T(8,128)} custom-call(bf16[128,512]{1,0:T(8,128)(2,1)} %k_ref.5, bf16[128,512]{1,0:T(8,128)(2,1)} %v_ref.5, f32[4,128]{1,0:T(4,128)} %decay_hbm.1), custom_call_target="tpu_custom_call" | custom-call | tf_op jit(solution)/shard_map/pallas_call | solution.py:325
  7.7 0.0 copy-start
  7.7 0.0 copy-start.1
  7.7 0.0 copy-start.2
  7.7 0.0 copy-start.3
  7.7 0.0 copy-start.5
  7.7 18.9 %all-to-all-start = ((f32[64,9,1,128]{3,2,1,0:T(1,128)}), f32[64,9,1,128]{3,2,1,0:T(1,128)S(1)}, u32[]{:S(2)}, u32[]{:S(2)}) async-start(f32[64,9,1,128]{3,2,1,0:T(1,128)} %bitcast.28), calls=%async_computation | async-start | bytes 589824 | tf_op jit(solution)/shard_map/all_to_all | solution.py:342
  26.6 0.0 copy-start.4
  26.6 0.0 copy-start.6
  26.7 0.6 copy-done.4
  27.3 0.6 shard_map.118
  27.9 16.3 %all-to-all-done = f32[64,9,1,128]{3,2,1,0:T(1,128)S(1)} async-done(((f32[64,9,1,128]{3,2,1,0:T(1,128)}), f32[64,9,1,128]{3,2,1,0:T(1,128)S(1)}, u32[]{:S(2)}, u32[]{:S(2)}) %all-to-all-start) | async-done | bytes 294944 | tf_op jit(solution)/shard_map/all_to_all | solution.py:342
  44.2 0.1 shard_map.120
  44.3 22.8 %all_to_all.30 = f32[64,8,1,128]{3,1,2,0:T(8,128)S(1)} all-to-all(f32[64,8,1,128]{3,1,2,0:T(8,128)S(1)} %bitcast.23), channel_id=1, replica_groups=mesh['tm'=64,'head'=8] {'tm'}, dimensions={0} | all-to-all | bytes 524288 | tf_op jit(solution)/shard_map/all_to_all | solution.py:342
  67.2 0.5 shard_map.121
  67.7 8.6 %all_to_all.31.sums_ref = f32[8,8,128]{2,1,0:T(8,128)S(1)} all-to-all(f32[8,8,128]{2,1,0:T(8,128)S(1)} %get-tuple-element.40), channel_id=1, replica_groups=mesh['tm'=64,'head'=8] {'head'}, dimensions={0} | all-to-all | bytes 65536 | tf_op jit(solution)/shard_map/all_to_all | solution.py:393
  76.3 4.5 %shard_map.122 = (f32[128,512]{1,0:T(8,128)S(1)}, f32[128,128]{1,0:T(8,128)S(1)}, f32[528,128]{1,0:T(8,128)S(1)}) custom-call(f32[8,8,128]{2,1,0:T(8,128)S(1)} %all_to_all.31.sums_ref, f32[128,512]{1,0:T(8,128)S(1)} %get-tuple-element.39.o_ref, bf16[128,512]{1,0:T(8,128)(2,1)S(1)} %copy-done, f32[128,128]{1,0:T(8,128)S(1)} %get-tuple-element.32.scales_ref, ...), custom_call_target="tpu_custom_call" | custom-call | tf_op jit(solution)/shard_map/pallas_call | solution.py:325
  80.9 21.0 %all_to_all.32 = f32[16,33,1,128]{3,2,1,0:T(1,128)S(1)} all-to-all(f32[16,33,1,128]{3,2,1,0:T(1,128)S(1)} %bitcast.22), channel_id=1, replica_groups={{0,8,16,24,32,40,48,56,64,72,80,88,96,104,112,120},{128,136,144,152,160..., dimensions={0} | all-to-all | bytes 540672 | tf_op jit(solution)/shard_map/all_to_all | solution.py:342
  101.9 8.1 %all_to_all.33 = f32[4,34,1,128]{3,2,1,0:T(1,128)S(1)} all-to-all(f32[4,34,1,128]{3,2,1,0:T(1,128)S(1)} %bitcast.24), channel_id=1, replica_groups={{0,128,256,384},{8,136,264,392},{16,144,272,400},{24,152,280,408},{32,1..., dimensions={0} | all-to-all | bytes 139264 | tf_op jit(solution)/shard_map/all_to_all | solution.py:342
  110.0 0.7 shard_map.125
  110.7 4.2 %all-to-all-start.5 = ((f32[16,33,1,128]{3,2,1,0:T(1,128)}), f32[16,33,1,128]{3,2,1,0:T(1,128)S(1)}, u32[]{:S(2)}, u32[]{:S(2)}) async-start(f32[16,33,1,128]{3,2,1,0:T(1,128)} %bitcast.11), calls=%async_computation.5 | async-start | bytes 540672 | tf_op jit(solution)/shard_map/all_to_all | solution.py:342
  114.9 2.0 %shard_map.123 = (bf16[128,512]{1,0:T(8,128)(2,1)}, bf16[128,512]{1,0:T(8,128)(2,1)}, f32[128,512]{1,0:T(8,128)S(1)}, f32[128,512]{1,0:T(8,128)S(1)}, f32[4,128]{1,0:T(4,128)S(1)}) custom-call(bf16[128,512]{1,0:T(8,128)(2,1)S(1)} %copy-done, bf16[128,512]{1,0:T(8,128)(2,1)S(1)} %copy-done.1, bf16[128,512]{1,0:T(8,128)(2,1)S(1)} %copy-done.2, ...), custom_call_target="tpu_custom_call" | custom-call | flops 40000000 | bytes 2000000 | tf_op jit(solution)/shard_map/pallas_call | solution.py:325
  116.9 14.1 %all-to-all-done.5 = f32[16,33,1,128]{3,2,1,0:T(1,128)S(1)} async-done(((f32[16,33,1,128]{3,2,1,0:T(1,128)}), f32[16,33,1,128]{3,2,1,0:T(1,128)S(1)}, u32[]{:S(2)}, u32[]{:S(2)}) %all-to-all-start.5) | async-done | bytes 270368 | tf_op jit(solution)/shard_map/all_to_all | solution.py:342
  131.0 1.1 shard_map.126
  (7 shorter events, 0.1 us)
Async XLA Ops:
  7.7 19.0 %copy-start = (bf16[128,512]{1,0:T(8,128)(2,1)S(1)}, bf16[128,512]{1,0:T(8,128)(2,1)}, u32[]{:S(2)}) copy-start(bf16[128,512]{1,0:T(8,128)(2,1)} %q_ref.7) | copy-start | bytes 393220
  7.7 19.0 %copy-start.1 = (bf16[128,512]{1,0:T(8,128)(2,1)S(1)}, bf16[128,512]{1,0:T(8,128)(2,1)}, u32[]{:S(2)}) copy-start(bf16[128,512]{1,0:T(8,128)(2,1)} %k_ref.5) | copy-start | bytes 393220
  7.7 19.0 %copy-start.2 = (bf16[128,512]{1,0:T(8,128)(2,1)S(1)}, bf16[128,512]{1,0:T(8,128)(2,1)}, u32[]{:S(2)}) copy-start(bf16[128,512]{1,0:T(8,128)(2,1)} %v_ref.5) | copy-start | bytes 393220
  7.7 19.0 %copy-start.3 = (bf16[128,512]{1,0:T(8,128)(2,1)S(1)}, bf16[128,512]{1,0:T(8,128)(2,1)}, u32[]{:S(2)}) copy-start(bf16[128,512]{1,0:T(8,128)(2,1)} %grad_ref.3) | copy-start | bytes 393220
  7.7 19.0 %copy-start.5 = (f32[512]{0:T(512)S(1)}, f32[512]{0:T(512)}, u32[]{:S(2)}) copy-start(f32[512]{0:T(512)} %param.12) | copy-start | bytes 6148
  7.7 36.5 %all-to-all-start = ((f32[64,9,1,128]{3,2,1,0:T(1,128)}), f32[64,9,1,128]{3,2,1,0:T(1,128)S(1)}, u32[]{:S(2)}, u32[]{:S(2)}) async-start(f32[64,9,1,128]{3,2,1,0:T(1,128)} %bitcast.28), calls=%async_computation | async-start | bytes 589824 | tf_op jit(solution)/shard_map/all_to_all | solution.py:342
  26.6 0.7 copy-start.4
  26.6 0.7 copy-start.6
  110.7 20.3 %all-to-all-start.5 = ((f32[16,33,1,128]{3,2,1,0:T(1,128)}), f32[16,33,1,128]{3,2,1,0:T(1,128)S(1)}, u32[]{:S(2)}, u32[]{:S(2)}) async-start(f32[16,33,1,128]{3,2,1,0:T(1,128)} %bitcast.11), calls=%async_computation.5 | async-start | bytes 540672 | tf_op jit(solution)/shard_map/all_to_all | solution.py:342

commit v5 on v4

--- a/solution.py
+++ b/solution.py
@@ -12,8 +12,8 @@
 WIDTH = 4096
 EPS = 1e-06
 CORES = 2
-STAGGER_FIRST_NS = 5000
-STAGGER_NS = 4000
+STAGGER_FIRST_NS = 4500
+STAGGER_NS = 3500
 SCALE = DK ** (-0.5)
 Z = 16
 Y = 4

time: 133 us -> 133 us (level)
  the two profiles are of different devices: /device:TPU:2 before, /device:TPU:32 now
where the time goes in v5:
time: 133 us; the launch traced here: 132 us
  blocking collectives  61.5 us (46%)
  waiting for transfers between devices  29.4 us (22%)
  starting transfers between devices  24.2 us (18%)
  Pallas kernels  15.8 us (12%)
    all_to_all x3, blocking collectives, exchange(): lax.all_to_all(value.reshape(peers, rows, 1, DK), 'tm', 0, 0, axis_index_...  52 us
    all_to_all x2, waiting for transfers between devices, exchange(): lax.all_to_all(value.reshape(peers, rows, 1, DK), 'tm', 0, 0, axis_index_...  29.4 us
    all_to_all x2, starting transfers between devices, exchange(): lax.all_to_all(value.reshape(peers, rows, 1, DK), 'tm', 0, 0, axis_index_...  24.2 us
    pallas_call x9, Pallas kernels, call(): pl.pallas_call(kernel, out_shape=[jax.ShapeDtypeStruct(s, d) for s, d in...  15.8 us
    all_to_all x1, blocking collectives, body(): sums = lax.all_to_all(sums, 'head', 0, 0, tiled=True)  9.55 us
  transfers between devices with their start and end apart: 2, of which 2 were waited for; matrix products, arithmetic and copies ran while one was open for 0% of the time, Pallas kernels for 2%

profile of v5, /device:TPU:32, one launch (start us, length us, event | category | flops | bytes accessed | tf_op | source)
XLA Modules:
  0.0 132.3 jit_solution(6885338751201509903)
XLA Ops:
  0.6 6.5 %shard_map.119 = f32[576,128]{1,0:T(8,128)} custom-call(bf16[128,512]{1,0:T(8,128)(2,1)} %k_ref.5, bf16[128,512]{1,0:T(8,128)(2,1)} %v_ref.5, f32[4,128]{1,0:T(4,128)} %decay_hbm.1), custom_call_target="tpu_custom_call" | custom-call | tf_op jit(solution)/shard_map/pallas_call | solution.py:325
  7.2 0.0 copy-start
  7.2 0.0 copy-start.1
  7.2 0.0 copy-start.2
  7.2 0.0 copy-start.3
  7.2 0.0 copy-start.5
  7.2 18.5 %all-to-all-start = ((f32[64,9,1,128]{3,2,1,0:T(1,128)}), f32[64,9,1,128]{3,2,1,0:T(1,128)S(1)}, u32[]{:S(2)}, u32[]{:S(2)}) async-start(f32[64,9,1,128]{3,2,1,0:T(1,128)} %bitcast.28), calls=%async_computation | async-start | bytes 589824 | tf_op jit(solution)/shard_map/all_to_all | solution.py:342
  25.8 0.0 copy-start.4
  25.8 0.0 copy-start.6
  25.9 0.6 copy-done.4
  26.5 0.6 shard_map.118
  27.1 16.0 %all-to-all-done = f32[64,9,1,128]{3,2,1,0:T(1,128)S(1)} async-done(((f32[64,9,1,128]{3,2,1,0:T(1,128)}), f32[64,9,1,128]{3,2,1,0:T(1,128)S(1)}, u32[]{:S(2)}, u32[]{:S(2)}) %all-to-all-start) | async-done | bytes 294944 | tf_op jit(solution)/shard_map/all_to_all | solution.py:342
  43.1 0.1 shard_map.120
  43.2 22.9 %all_to_all.30 = f32[64,8,1,128]{3,1,2,0:T(8,128)S(1)} all-to-all(f32[64,8,1,128]{3,1,2,0:T(8,128)S(1)} %bitcast.23), channel_id=1, replica_groups=mesh['tm'=64,'head'=8] {'tm'}, dimensions={0} | all-to-all | bytes 524288 | tf_op jit(solution)/shard_map/all_to_all | solution.py:342
  66.2 0.5 shard_map.121
  66.7 9.6 %all_to_all.31.sums_ref = f32[8,8,128]{2,1,0:T(8,128)S(1)} all-to-all(f32[8,8,128]{2,1,0:T(8,128)S(1)} %get-tuple-element.40), channel_id=1, replica_groups=mesh['tm'=64,'head'=8] {'head'}, dimensions={0} | all-to-all | bytes 65536 | tf_op jit(solution)/shard_map/all_to_all | solution.py:393
  76.3 4.0 %shard_map.122 = (f32[128,512]{1,0:T(8,128)S(1)}, f32[128,128]{1,0:T(8,128)S(1)}, f32[528,128]{1,0:T(8,128)S(1)}) custom-call(f32[8,8,128]{2,1,0:T(8,128)S(1)} %all_to_all.31.sums_ref, f32[128,512]{1,0:T(8,128)S(1)} %get-tuple-element.39.o_ref, bf16[128,512]{1,0:T(8,128)(2,1)S(1)} %copy-done, f32[128,128]{1,0:T(8,128)S(1)} %get-tuple-element.32.scales_ref, ...), custom_call_target="tpu_custom_call" | custom-call | tf_op jit(solution)/shard_map/pallas_call | solution.py:325
  80.3 21.0 %all_to_all.32 = f32[16,33,1,128]{3,2,1,0:T(1,128)S(1)} all-to-all(f32[16,33,1,128]{3,2,1,0:T(1,128)S(1)} %bitcast.22), channel_id=1, replica_groups={{0,8,16,24,32,40,48,56,64,72,80,88,96,104,112,120},{128,136,144,152,160..., dimensions={0} | all-to-all | bytes 540672 | tf_op jit(solution)/shard_map/all_to_all | solution.py:342
  101.3 8.0 %all_to_all.33 = f32[4,34,1,128]{3,2,1,0:T(1,128)S(1)} all-to-all(f32[4,34,1,128]{3,2,1,0:T(1,128)S(1)} %bitcast.24), channel_id=1, replica_groups={{0,128,256,384},{8,136,264,392},{16,144,272,400},{24,152,280,408},{32,1..., dimensions={0} | all-to-all | bytes 139264 | tf_op jit(solution)/shard_map/all_to_all | solution.py:342
  109.4 0.7 shard_map.125
  110.1 5.7 %all-to-all-start.5 = ((f32[16,33,1,128]{3,2,1,0:T(1,128)}), f32[16,33,1,128]{3,2,1,0:T(1,128)S(1)}, u32[]{:S(2)}, u32[]{:S(2)}) async-start(f32[16,33,1,128]{3,2,1,0:T(1,128)} %bitcast.11), calls=%async_computation.5 | async-start | bytes 540672 | tf_op jit(solution)/shard_map/all_to_all | solution.py:342
  115.8 2.0 %shard_map.123 = (bf16[128,512]{1,0:T(8,128)(2,1)}, bf16[128,512]{1,0:T(8,128)(2,1)}, f32[128,512]{1,0:T(8,128)S(1)}, f32[128,512]{1,0:T(8,128)S(1)}, f32[4,128]{1,0:T(4,128)S(1)}) custom-call(bf16[128,512]{1,0:T(8,128)(2,1)S(1)} %copy-done, bf16[128,512]{1,0:T(8,128)(2,1)S(1)} %copy-done.1, bf16[128,512]{1,0:T(8,128)(2,1)S(1)} %copy-done.2, ...), custom_call_target="tpu_custom_call" | custom-call | flops 40000000 | bytes 2000000 | tf_op jit(solution)/shard_map/pallas_call | solution.py:325
  117.8 13.4 %all-to-all-done.5 = f32[16,33,1,128]{3,2,1,0:T(1,128)S(1)} async-done(((f32[16,33,1,128]{3,2,1,0:T(1,128)}), f32[16,33,1,128]{3,2,1,0:T(1,128)S(1)}, u32[]{:S(2)}, u32[]{:S(2)}) %all-to-all-start.5) | async-done | bytes 270368 | tf_op jit(solution)/shard_map/all_to_all | solution.py:342
  131.2 1.1 shard_map.126
  (7 shorter events, 0.1 us)
Async XLA Ops:
  7.2 18.6 %copy-start = (bf16[128,512]{1,0:T(8,128)(2,1)S(1)}, bf16[128,512]{1,0:T(8,128)(2,1)}, u32[]{:S(2)}) copy-start(bf16[128,512]{1,0:T(8,128)(2,1)} %q_ref.7) | copy-start | bytes 393220
  7.2 18.6 %copy-start.1 = (bf16[128,512]{1,0:T(8,128)(2,1)S(1)}, bf16[128,512]{1,0:T(8,128)(2,1)}, u32[]{:S(2)}) copy-start(bf16[128,512]{1,0:T(8,128)(2,1)} %k_ref.5) | copy-start | bytes 393220
  7.2 18.6 %copy-start.2 = (bf16[128,512]{1,0:T(8,128)(2,1)S(1)}, bf16[128,512]{1,0:T(8,128)(2,1)}, u32[]{:S(2)}) copy-start(bf16[128,512]{1,0:T(8,128)(2,1)} %v_ref.5) | copy-start | bytes 393220
  7.2 18.6 %copy-start.3 = (bf16[128,512]{1,0:T(8,128)(2,1)S(1)}, bf16[128,512]{1,0:T(8,128)(2,1)}, u32[]{:S(2)}) copy-start(bf16[128,512]{1,0:T(8,128)(2,1)} %grad_ref.3) | copy-start | bytes 393220
  7.2 18.6 %copy-start.5 = (f32[512]{0:T(512)S(1)}, f32[512]{0:T(512)}, u32[]{:S(2)}) copy-start(f32[512]{0:T(512)} %param.12) | copy-start | bytes 6148
  7.2 35.8 %all-to-all-start = ((f32[64,9,1,128]{3,2,1,0:T(1,128)}), f32[64,9,1,128]{3,2,1,0:T(1,128)S(1)}, u32[]{:S(2)}, u32[]{:S(2)}) async-start(f32[64,9,1,128]{3,2,1,0:T(1,128)} %bitcast.28), calls=%async_computation | async-start | bytes 589824 | tf_op jit(solution)/shard_map/all_to_all | solution.py:342
  25.8 0.7 copy-start.4
  25.8 0.7 copy-start.6
  110.1 21.1 %all-to-all-start.5 = ((f32[16,33,1,128]{3,2,1,0:T(1,128)}), f32[16,33,1,128]{3,2,1,0:T(1,128)S(1)}, u32[]{:S(2)}, u32[]{:S(2)}) async-start(f32[16,33,1,128]{3,2,1,0:T(1,128)} %bitcast.11), calls=%async_computation.5 | async-start | bytes 540672 | tf_op jit(solution)/shard_map/all_to_all | solution.py:342
